TPU v7x, 128 devices: a whole 4x4x4 slice. The times are simulated.
128 devices in a mesh: cell: 16 (over z, y_hi, core), vel: 8 (over y_lo, x).
Axes of the slice: x: 4, y: 4 (y_hi: 2, y_lo: 2; y = y_hi * 2 + y_lo), z: 4, core: 2. Of those that a mesh axis runs over, the one named last changes fastest.
Arguments:
- distribution: float32 [128, 128, 4096], P(None, 'cell', 'vel'), may hold values from 0.2 to 2
- cell_type: int32 [128, 128], P(None, 'cell'), may hold values from 0 to 2, as said below
- first_kernel: float32 [16, 4096], replicated, may hold values from -1.5 to 1.5
- second_kernel: float32 [16, 4096], replicated, may hold values from -1.5 to 1.5
- loss_kernel: float32 [4096], replicated, may hold values from -4 to 4
Outputs:
- updated: float32 [128, 128, 4096], P(None, 'cell', 'vel')
Inputs may be any that keep to these rules, and one draw needn't show every extreme that they name: `cell_type`: cells with x = 0, x = 127 or y = 0 are 1, the other cells with y = 127 are 2, and every other cell is 1 with probability 1/40, else 0.
All inputs are finite; a program needn't handle non-finite values.
Results may differ from a plain program's by a relative error of at most 0.0004.
Values sent between devices are 32-bit elements; how exact they have to be, the bound alone decides.
A program may use at most 128 MiB of HBM per device.

v0:
```python
import math

import jax
import jax.numpy as jnp
from jax import lax
from jax.sharding import PartitionSpec as P

NVEL = 16
DIRS = 16


courant = 0.45
collision_timestep = 0.1
pass_forms = ("ai,ijkc->ajkc", "aj,ijkc->iakc", "ak,ijkc->ijac")


def copy_for_each(value, axis):
    length = lax.axis_size(axis)
    return lax.all_to_all(
        jnp.broadcast_to(value[None], (length, *value.shape)), axis, 0, 0, tiled=True
    )


def of_everyone(value, axis):
    everything = copy_for_each(value, axis)
    return jnp.sum(everything, axis=0)


def padded_2(cells, sides, width):
    for axis, dim in sides:
        count = lax.axis_size(axis)
        ends = count - 1
        head = lax.slice_in_dim(cells, 0, width, axis=dim)
        tail = lax.slice_in_dim(cells, cells.shape[dim] - width, cells.shape[dim], axis=dim)
        cells = jnp.concatenate(
            [
                lax.ppermute(tail, axis, [(i, (i + 1) % count) for i in range(ends)]),
                cells,
                lax.ppermute(head, axis, [((i + 1) % count, i) for i in range(ends)]),
            ],
            axis=dim,
        )
    return cells


def in_blocks(value, dim, length):
    dims = value.shape
    pieces = value.reshape(*dims[:dim], length, dims[dim] // length, *dims[dim + 1 :])
    return jnp.moveaxis(pieces, dim, 0)


def edges_of(length, count):
    step = length // count
    if step >= 8:
        step -= step % 8
    return [step * k for k in range(1, count)]


def in_order(pieces, dim):
    pieces = jnp.moveaxis(pieces, 0, dim)
    dims = pieces.shape
    return pieces.reshape(*dims[:dim], dims[dim] * dims[dim + 1], *dims[dim + 2 :])


def cut_exchange(value, axis, pieces, split_dim, concat_dim):
    blocks = in_blocks(value, split_dim, lax.axis_size(axis))
    split_at = max(range(1, max(2, blocks.ndim - 1)), key=lambda d: blocks.shape[d])
    outs = []
    for piece in jnp.split(blocks, edges_of(blocks.shape[split_at], pieces), axis=split_at):
        if piece.size:
            outs.append(lax.all_to_all(piece, axis, split_axis=0, concat_axis=0, tiled=True))
    return in_order(jnp.concatenate(outs, axis=split_at), concat_dim)


def components(nvel):
    levels = (2.0 * jnp.arange(nvel, dtype=jnp.float32) - (nvel - 1)) / (nvel - 1)
    along_x = jnp.repeat(levels, nvel * nvel)
    along_y = jnp.tile(jnp.repeat(levels, nvel), nvel)
    along_z = jnp.tile(levels, nvel * nvel)
    return (along_x, along_y, along_z)


def wall_tables(along_x, along_y, along_z):
    still_wall = jnp.exp(-4.5 * (along_x * along_x + along_y * along_y + along_z * along_z))
    still_wall = still_wall / jnp.sum(still_wall)
    moving = jnp.exp(
        -0.5 * ((3.0 * along_x - 1.0) ** 2 + 9.0 * along_y * along_y + 9.0 * along_z * along_z)
    )
    moving = moving / jnp.sum(moving)
    return (still_wall, moving)


def fourier_tables(nvel):
    indices = jnp.arange(nvel, dtype=jnp.int32)
    angles = 2.0 * math.pi * (indices[:, None] * indices[None, :] % nvel).astype(jnp.float32) / nvel
    cosine = jnp.cos(angles)
    sine_part = jnp.sin(angles)
    return (
        cosine.astype(jnp.bfloat16),
        (-sine_part).astype(jnp.bfloat16),
        (cosine / nvel).astype(jnp.bfloat16),
        (sine_part / nvel).astype(jnp.bfloat16),
    )


def apply_table(matrix, operand, pattern):
    return jnp.einsum(pattern, matrix, operand, preferred_element_type=jnp.float32)


def real_pass(operand, cos_table, sin_table, pattern):
    return (
        apply_table(cos_table, operand, pattern).astype(jnp.bfloat16),
        apply_table(sin_table, operand, pattern).astype(jnp.bfloat16),
    )


def complex_pass(real_part, imag_part, cos_table, sin_table, pattern):
    new_real = apply_table(cos_table, real_part, pattern) - apply_table(
        sin_table, imag_part, pattern
    )
    new_imag = apply_table(cos_table, imag_part, pattern) + apply_table(
        sin_table, real_part, pattern
    )
    return (new_real.astype(jnp.bfloat16), new_imag.astype(jnp.bfloat16))


def last_pass(real_part, imag_part, cos_table, sin_table, pattern):
    return apply_table(cos_table, real_part, pattern) - apply_table(sin_table, imag_part, pattern)


def spectrum_of(rounded, tables):
    real_part, imag_part = real_pass(rounded, tables[0], tables[1], pass_forms[0])
    real_part, imag_part = complex_pass(real_part, imag_part, tables[0], tables[1], pass_forms[1])
    return complex_pass(real_part, imag_part, tables[0], tables[1], pass_forms[2])


def inverse_of(kernel, spec_real, spec_imag, tables):
    weight = kernel[..., None]
    real_part = (weight * spec_real).astype(jnp.bfloat16)
    imag_part = (weight * spec_imag).astype(jnp.bfloat16)
    real_part, imag_part = complex_pass(real_part, imag_part, tables[2], tables[3], pass_forms[0])
    real_part, imag_part = complex_pass(real_part, imag_part, tables[2], tables[3], pass_forms[1])
    return last_pass(real_part, imag_part, tables[2], tables[3], pass_forms[2])


def collide(moved_block, kern_first, kern_second, kern_loss, tables):
    rounded = moved_block.astype(jnp.bfloat16)
    spec_real, spec_imag = spectrum_of(rounded, tables)

    def add_direction(direction, running):
        return running + inverse_of(
            kern_first[direction], spec_real, spec_imag, tables
        ) * inverse_of(kern_second[direction], spec_real, spec_imag, tables)

    gain = lax.fori_loop(
        0, kern_first.shape[0], add_direction, jnp.zeros(moved_block.shape, jnp.float32)
    )
    return gain - moved_block * inverse_of(kern_loss, spec_real, spec_imag, tables)


def transport(padded, along_x, along_y):
    center = padded[1:-1, 1:-1]
    back_x = center - padded[:-2, 1:-1]
    front_x = padded[2:, 1:-1] - center
    back_y = center - padded[1:-1, :-2]
    front_y = padded[1:-1, 2:] - center
    plus_x = jnp.maximum(along_x, 0.0)[None, None, :]
    minus_x = jnp.minimum(along_x, 0.0)[None, None, :]
    plus_y = jnp.maximum(along_y, 0.0)[None, None, :]
    minus_y = jnp.minimum(along_y, 0.0)[None, None, :]
    return -courant * (plus_x * back_x + minus_x * front_x + plus_y * back_y + minus_y * front_y)


def on_device(distribution, cell_type, first_kernel, second_kernel, loss_kernel):
    all_rows, cell_cols, block_vel = distribution.shape
    groups = lax.axis_size("vel")
    rank = lax.axis_index("vel")
    sub_rows = all_rows // groups
    along_x, along_y, along_z = components(NVEL)
    still_wall, moving = wall_tables(along_x, along_y, along_z)
    sub_type = lax.dynamic_slice_in_dim(cell_type, rank * sub_rows, sub_rows, 0)
    local_fluid_cells = sub_type == 0
    first_vel = rank * block_vel
    here_x = lax.dynamic_slice_in_dim(along_x, first_vel, block_vel)
    here_y = lax.dynamic_slice_in_dim(along_y, first_vel, block_vel)
    still_here = lax.dynamic_slice_in_dim(still_wall, first_vel, block_vel)
    moving_here = lax.dynamic_slice_in_dim(moving, first_vel, block_vel)
    density = of_everyone(jnp.sum(distribution, axis=2), "vel")
    fluid_cell_mask = cell_type == 0
    thermal = density[:, :, None] * jnp.where(
        cell_type[:, :, None] == 1, still_here[None, None, :], moving_here[None, None, :]
    )
    walled = jnp.where(fluid_cell_mask[:, :, None], distribution, thermal)
    rimmed = padded_2(walled, (("cell", 1),), 1)
    padded = jnp.pad(rimmed, ((1, 1), (0, 0), (0, 0)))
    increment = transport(padded, here_x, here_y)
    moved = jnp.where(fluid_cell_mask[:, :, None], walled + increment, walled)
    velocity_grids = lax.all_to_all(moved, "vel", split_axis=0, concat_axis=2, tiled=True)
    vel_count = velocity_grids.shape[2]
    tables = fourier_tables(NVEL)
    cell_block = velocity_grids.transpose(2, 0, 1).reshape(NVEL, NVEL, NVEL, sub_rows * cell_cols)
    kern_first = first_kernel.reshape(DIRS, NVEL, NVEL, NVEL)
    kern_second = second_kernel.reshape(DIRS, NVEL, NVEL, NVEL)
    kern_loss = loss_kernel.reshape(NVEL, NVEL, NVEL)
    collision_operator = collide(cell_block, kern_first, kern_second, kern_loss, tables)
    collision_operator = collision_operator.reshape(vel_count, sub_rows, cell_cols).transpose(
        1, 2, 0
    )
    completed_state = jnp.where(
        local_fluid_cells[:, :, None],
        velocity_grids + collision_timestep * collision_operator,
        velocity_grids,
    )
    return cut_exchange(completed_state, "vel", 2, 2, 0)


def solution(mesh):
    return jax.shard_map(
        on_device,
        mesh=mesh,
        in_specs=(P(None, "cell", "vel"), P(None, "cell"), P(), P(), P()),
        out_specs=P(None, "cell", "vel"),
        check_vma=False,
    )
```

profile of v0, /device:TPU:33, one launch (start us, length us, event | category | flops | bytes accessed | tf_op | source)
XLA Modules:
  0.0 597.1 jit_solution(4058882469202572058)
XLA Ops:
  0.0 2.0 reduce_sum.36
  2.7 5.0 all-to-all-start
  10.2 2.6 all-to-all-done
  14.2 6.5 %collective-permute-start = (f32[128,1,512]{2,0,1:T(8,128)S(1)}, f32[128,1,512]{2,0,1:T(8,128)S(1)}, u32[]{:S(2)}, u32[]{:S(2)}) collective-permute-start(f32[128,1,512]{2,0,1:T(8,128)S(1)} %get-tuple-element.315), channel_id=1, source_target_pairs={{0,8},{8,16},{16,24},{24,32},{32,40},{40,48},{48,56},{56,64},{64,7... | collective-permute-start | bytes 786440 | tf_op jit(solution)/shard_map/ppermute | solution.py:37
  20.7 1.9 collective-permute-start.1
  22.7 1.4 collective-permute-done
  24.0 5.9 collective-permute-done.1
  31.7 2.5 copy.192
  34.2 3.9 all-to-all-start.1
  39.0 2.0 reshape.52
  41.1 2.1 reshape.54
  43.2 20.9 %all-to-all-done.1 = f32[128,8,512]{2,1,0:T(8,128)S(1)} async-done(((f32[128,8,512]{2,1,0:T(8,128)}), f32[128,8,512]{2,1,0:T(8,128)S(1)}, u32[]{:S(2)}, u32[]{:S(2)}) %all-to-all-start.1) | async-done | bytes 2097184 | tf_op jit(solution)/shard_map/all_to_all | solution.py:198
  64.0 3.0 copy.298
  67.0 1.7 all_to_all.26
  68.7 9.0 %reshape.53 = f32[16,16,16,128]{2,1,0,3:T(8,128)} reshape(f32[4096,16,8]{0,2,1:T(8,128)S(1)} %bitcast.211) | data formatting | bytes 4194304 | tf_op jit(solution)/shard_map/reshape | solution.py:201
  77.7 11.1 %copy.194 = bf16[16,16,16,128]{3,0,2,1:T(8,128)(2,1)S(1)} copy(f32[16,16,16,128]{2,1,0,3:T(8,128)} %reshape.53) | data formatting | bytes 3145728 | tf_op jit(solution)/shard_map/reshape | solution.py:201
  88.8 13.5 %copy.217 = f32[16,16,16,128]{3,2,1,0:T(8,128)} copy(f32[16,16,16,128]{2,1,0,3:T(8,128)} %reshape.53) | data formatting | bytes 4194304 | tf_op jit(solution)/shard_map/reshape | solution.py:201
  105.8 1.4 fusion.188
  107.2 1.4 fusion.189
  110.8 1.8 multiply_convert_fusion.2
  113.3 396.1 %while.15 = (s32[]{:T(128)}, f32[16,16,16,128]{3,2,1,0:T(8,128)}, f32[16,16,16,16]{3,2,1,0:T(8,128)}, bf16[16,16,16,128]{3,0,2,1:T(8,128)(2,1)S(1)}, bf16[16,16,...) while((s32[]{:T(128)}, f32[16,16,16,128]{3,2,1,0:T(8,128)}, ...), condition=%wide.region_5.6_spmd.clone.clone, body=%wide.region_4.5_spmd.clone.clone.sunk | while | flops 359219200 | bytes 96731296 | solution.py:155
  134.5 1.4 fusion.472
  144.2 1.4 fusion.465
  168.2 1.4 fusion.465
  182.4 1.4 fusion.472
  192.1 1.4 fusion.465
  216.1 1.4 fusion.465
  230.3 1.4 fusion.472
  240.0 1.4 fusion.465
  264.0 1.4 fusion.465
  278.2 1.4 fusion.472
  287.9 1.4 fusion.465
  311.9 1.4 fusion.465
  326.1 1.4 fusion.472
  335.8 1.4 fusion.465
  359.8 1.4 fusion.465
  374.1 1.4 fusion.472
  479.6 1.4 fusion.465
  503.5 1.4 fusion.465
  520.7 13.5 %copy.218 = f32[16,16,16,128]{2,1,0,3:T(8,128)} copy(f32[16,16,16,128]{3,2,1,0:T(8,128)S(1)} %fusion.187) | data formatting | bytes 4194304 | tf_op jit(solution)/shard_map/mul | solution.py:211
  534.1 15.6 %mul.561 = f32[4096,16,8]{0,2,1:T(8,128)} reshape(f32[16,16,16,128]{2,1,0,3:T(8,128)} %copy.218) | data formatting | bytes 4194304 | tf_op jit(solution)/shard_map/mul | solution.py:211
  549.7 1.9 add_select_fusion.1
  551.6 1.6 copy.297
  553.5 1.6 copy.219
  555.1 6.2 %all-to-all-start.2 = ((f32[8,8,8,512]{3,2,1,0:T(8,128)}), f32[8,8,8,512]{3,2,1,0:T(8,128)S(1)}, u32[]{:S(2)}, u32[]{:S(2)}) async-start(f32[8,8,8,512]{3,2,1,0:T(8,128)} %copy.219), calls=%async_computation.2 | async-start | bytes 2097152 | tf_op jit(solution)/shard_map/all_to_all | solution.py:71
  561.8 15.5 %all-to-all-done.2 = f32[8,8,8,512]{3,2,1,0:T(8,128)S(1)} async-done(((f32[8,8,8,512]{3,2,1,0:T(8,128)}), f32[8,8,8,512]{3,2,1,0:T(8,128)S(1)}, u32[]{:S(2)}, u32[]{:S(2)}) %all-to-all-start.2) | async-done | bytes 1048608 | tf_op jit(solution)/shard_map/all_to_all | solution.py:71
  577.4 17.7 %all_to_all.33 = f32[8,8,8,512]{3,2,1,0:T(8,128)S(1)} all-to-all(f32[8,8,8,512]{3,2,1,0:T(8,128)S(1)} %copy.220), channel_id=1, replica_groups=mesh['cell'=16,'vel'=8] {'vel'}, dimensions={0} | all-to-all | bytes 2097152 | tf_op jit(solution)/shard_map/all_to_all | solution.py:71
  595.1 1.6 pad_maximum_fusion.2
  (487 shorter events, 382.9 us)
Async XLA Ops:
  0.0 12.8 %copy-start.6 = (f32[128,8,512]{2,1,0:T(8,128)S(1)}, f32[128,8,512]{2,1,0:T(8,128)}, u32[]{:S(2)}) copy-start(f32[128,8,512]{2,1,0:T(8,128)} %param.7) | copy-start | bytes 6291460
  0.0 8.0 %copy-start.11 = (s32[128,8]{0,1:T(8,128)S(1)}, s32[128,8]{0,1:T(8,128)}, u32[]{:S(2)}) copy-start(s32[128,8]{0,1:T(8,128)} %param.8) | copy-start | bytes 12292
  2.7 10.1 %all-to-all-start = ((f32[8,128,8]{1,2,0:T(8,128)}), f32[8,128,8]{1,2,0:T(8,128)S(1)}, u32[]{:S(2)}, u32[]{:S(2)}) async-start(f32[8,128,8]{1,2,0:T(8,128)} %broadcast_in_dim.89), calls=%async_computation | async-start | bytes 65536 | tf_op jit(solution)/shard_map/all_to_all | solution.py:19
  14.2 9.8 %collective-permute-start = (f32[128,1,512]{2,0,1:T(8,128)S(1)}, f32[128,1,512]{2,0,1:T(8,128)S(1)}, u32[]{:S(2)}, u32[]{:S(2)}) collective-permute-start(f32[128,1,512]{2,0,1:T(8,128)S(1)} %get-tuple-element.315), channel_id=1, source_target_pairs={{0,8},{8,16},{16,24},{24,32},{32,40},{40,48},{48,56},{56,64},{64,7... | collective-permute-start | bytes 786440 | tf_op jit(solution)/shard_map/ppermute | solution.py:37
  20.7 9.2 %collective-permute-start.1 = (f32[128,1,512]{2,0,1:T(8,128)S(1)}, f32[128,1,512]{2,0,1:T(8,128)S(1)}, u32[]{:S(2)}, u32[]{:S(2)}) collective-permute-start(f32[128,1,512]{2,0,1:T(8,128)S(1)} %get-tuple-element.316), channel_id=1, source_target_pairs={{8,0},{16,8},{24,16},{32,24},{40,32},{48,40},{56,48},{64,56},{72,6... | collective-permute-start | bytes 786440 | tf_op jit(solution)/shard_map/ppermute | solution.py:39
  34.2 4.7 copy-start.10
  34.2 4.8 copy-start.8
  34.2 29.8 %all-to-all-start.1 = ((f32[128,8,512]{2,1,0:T(8,128)}), f32[128,8,512]{2,1,0:T(8,128)S(1)}, u32[]{:S(2)}, u32[]{:S(2)}) async-start(f32[128,8,512]{2,1,0:T(8,128)} %copy.192), calls=%async_computation.1 | async-start | bytes 4194304 | tf_op jit(solution)/shard_map/all_to_all | solution.py:198
  38.2 2.9 copy-start.9
  68.7 9.0 %copy-start.3 = (f32[16,8,4096]{2,1,0:T(8,128)}, f32[16,8,4096]{2,1,0:T(8,128)S(1)}, u32[]{:S(2)}) copy-start(f32[16,8,4096]{2,1,0:T(8,128)S(1)} %all_to_all.26) | copy-start | bytes 6291460
  145.6 1.6 copy-start
  148.5 1.4 copy-start.1
  169.5 1.6 copy-start
  172.5 1.4 copy-start.1
  193.5 1.6 copy-start
  196.4 1.4 copy-start.1
  217.4 1.6 copy-start
  220.4 1.4 copy-start.1
  241.4 1.6 copy-start
  244.3 1.4 copy-start.1
  265.3 1.6 copy-start
  268.3 1.4 copy-start.1
  289.3 1.6 copy-start
  292.3 1.4 copy-start.1
  313.2 1.6 copy-start
  316.2 1.4 copy-start.1
  337.2 1.6 copy-start
  340.2 1.4 copy-start.1
  361.2 1.6 copy-start
  364.1 1.4 copy-start.1
  385.1 1.6 copy-start
  388.1 1.4 copy-start.1
  409.1 1.6 copy-start
  412.0 1.4 copy-start.1
  433.0 1.6 copy-start
  436.0 1.4 copy-start.1
  457.0 1.6 copy-start
  459.9 1.4 copy-start.1
  480.9 1.6 copy-start
  483.9 1.4 copy-start.1
  504.9 1.6 copy-start
  507.8 1.4 copy-start.1
  509.4 1.2 copy-start.5
  517.0 1.9 copy-start.7
  518.4 1.6 copy-start.2
  534.1 15.6 %copy-start.4 = (f32[16,8,4096]{2,1,0:T(8,128)S(1)}, f32[16,8,4096]{2,1,0:T(8,128)}, u32[]{:S(2)}) copy-start(f32[16,8,4096]{2,1,0:T(8,128)} %copy-done.3) | copy-start | bytes 6291460
  534.1 15.6 %copy-start.12 = (pred[16,8]{1,0:T(8,128)(4,1)S(1)}, pred[16,8]{1,0:T(8,128)(4,1)}, u32[]{:S(2)}) copy-start(pred[16,8]{1,0:T(8,128)(4,1)} %copy.189) | copy-start | bytes 388
  555.1 22.3 %all-to-all-start.2 = ((f32[8,8,8,512]{3,2,1,0:T(8,128)}), f32[8,8,8,512]{3,2,1,0:T(8,128)S(1)}, u32[]{:S(2)}, u32[]{:S(2)}) async-start(f32[8,8,8,512]{3,2,1,0:T(8,128)} %copy.219), calls=%async_computation.2 | async-start | bytes 2097152 | tf_op jit(solution)/shard_map/all_to_all | solution.py:71
where the time goes:
time: 604 us; the launch traced here: 597 us
  matrix products  343 us (57%)
  local copies, waits for them, and re-layouts  142 us (24%)
  waiting for transfers between devices  46.2 us (8%)
  starting transfers between devices  23.6 us (4%)
  blocking collectives  17.7 us (3%)
  loops' own time  14.1 us (2%)
  other arithmetic  10.6 us (2%)
    dot_general x340, matrix products, apply_table(): jnp.einsum(pattern, matrix, operand, preferred_element_type=jnp.float32)  343 us
    while x64, local copies, waits for them, and re-layouts  39.2 us
    reshape x3, local copies, waits for them, and re-layouts, on_device(): velocity_grids.transpose(2, 0, 1)  33.5 us
    mul x2, local copies, waits for them, and re-layouts, on_device(): collision_timestep * collision_operator  29.1 us
    all_to_all x1, waiting for transfers between devices, on_device(): lax.all_to_all(moved, 'vel', split_axis=0, concat_axis=2, tiled=True)  20.9 us
    all_to_all x1, blocking collectives, cut_exchange(): lax.all_to_all(piece, axis, split_axis=0, concat_axis=0, tiled=True)  17.7 us
    dynamic_slice x32, local copies, waits for them, and re-layouts, add_direction(): kern_second[direction]  17.6 us
    all_to_all x1, waiting for transfers between devices, cut_exchange(): lax.all_to_all(piece, axis, split_axis=0, concat_axis=0, tiled=True)  15.5 us
  transfers between devices with their start and end apart: 5, of which 5 were waited for; matrix products, arithmetic and copies ran while one was open for 1% of the time, Pallas kernels for 0%

commit v1 on v0

v1 whole, which is shorter than its diff:
```python
import functools

import jax
import jax.numpy as jnp
import numpy as np
from jax import lax
from jax.experimental import pallas as pl
from jax.experimental.pallas import tpu as pltpu
from jax.sharding import PartitionSpec as P

N = 16
DIRS = 16
courant = 0.45
collision_timestep = 0.1
NN = (((1,), (0,)), ((), ()))
NT = (((1,), (1,)), ((), ()))
F32 = jnp.float32
BF16 = jnp.bfloat16


def bf16_values(values):
    return np.asarray(values, np.float32).astype(BF16).astype(np.float64)


def line_tables():
    n = np.arange(N)
    angle = 2 * np.pi * (n[:, None] * n[None, :] % N) / N
    c, s = np.cos(angle), np.sin(angle)
    return bf16_values(c), bf16_values(-s), bf16_values(c / N), bf16_values(s / N)


def column_of(row, slot):
    if slot == 0:
        return row % 8, 0 if row < 8 else 8
    return row, slot


def j_table(fr, fi):
    eye = np.eye(N)
    real, imag = np.kron(fr, eye), np.kron(fi, eye)
    return np.block([[real, -imag], [imag, real]])


def k_tables(fr, fi):
    out = np.zeros((4, N, N, 2, N, N))
    for kind in range(4):
        for row in range(N):
            for slot in range(8):
                b, c = column_of(row, slot)
                if slot == 0 and b == 0 and kind in (0, 2):
                    first = 0 if kind == 0 else 8
                    out[kind, row, 0, 0, first] = fr[c]
                    out[kind, row, 8, 0, 8 - first] = fr[c]
                    continue
                if slot == 0 and b == 0 and kind == 3:
                    b = 8
                if kind < 3:
                    out[kind, row, slot, 0, b], out[kind, row, slot, 1, b] = fr[c], -fi[c]
                    out[kind, row, 8 + slot, 0, b], out[kind, row, 8 + slot, 1, b] = fi[c], fr[c]
                else:
                    m = (N - b) % N
                    out[kind, row, slot, 0, m], out[kind, row, slot, 1, m] = fr[c], fi[c]
                    out[kind, row, 8 + slot, 0, m], out[kind, row, 8 + slot, 1, m] = fi[c], -fr[c]
    return out.reshape(4, 256, 512)


def inverse_i_tables(ir, ii):
    out = np.zeros((2, N, N, N, N))
    for kind in range(2):
        for slot in range(8):
            im = 8 + slot
            if kind == 1 and slot == 0:
                out[1, :, 0, 0, 0], out[1, :, 0, 8, 8] = ir[:, 0], ir[:, 8]
                out[1, :, 8, 0, 8], out[1, :, 8, 8, 0] = ir[:, 0], ir[:, 8]
                for a in range(1, 8):
                    out[1, :, 0, a, 0], out[1, :, 0, a, 8] = 2 * ir[:, a], -2 * ii[:, a]
                    h = 8 + a
                    out[1, :, 8, h, 0], out[1, :, 8, h, 8] = 2 * ir[:, h], -2 * ii[:, h]
                continue
            out[kind, :, slot, :, slot], out[kind, :, slot, :, im] = ir, -ii
            out[kind, :, im, :, im], out[kind, :, im, :, slot] = ir, ii
    return out.reshape(2, 256, 256)


def inverse_jk_table(ir, ii):
    real = np.einsum("jb,kc->bcjk", ir, ir) - np.einsum("jb,kc->bcjk", ii, ii)
    imag = np.einsum("jb,kc->bcjk", ir, ii) + np.einsum("jb,kc->bcjk", ii, ir)
    out = np.zeros((N, N, N, N))
    for row in range(N):
        for slot in range(8):
            b, c = column_of(row, slot)
            if slot == 0 and b == 0:
                out[:, :, row, 0], out[:, :, row, 8] = real[0, c], real[8, c]
            else:
                out[:, :, row, slot], out[:, :, row, 8 + slot] = 2 * real[b, c], -2 * imag[b, c]
    return out.reshape(256, 256)


def packing_index():
    out = np.zeros((4, 2, 256), np.int32)
    for kind in range(4):
        for row in range(N):
            for slot in range(8):
                for part in range(2):
                    b, c = column_of(row, slot)
                    if slot == 0 and b == 0:
                        b = (8 * part, 0, 8 * (1 - part), 8)[kind]
                    place = row * 16 + 8 * part + slot
                    out[kind, 0, place] = b * 16 + c
                    out[kind, 1, place] = (N - b) % N * 16 + (N - c) % N
    return out


def kind_of(a):
    return 0 if a == 0 else 1 if a < 8 else 2 if a == 8 else 3


def pack_body(first_ref, second_ref, loss_ref, index_ref, out_ref, all_ref, mid_ref, table_ref):
    for kind in range(4):
        for side in range(2):
            source = lax.broadcasted_iota(jnp.int32, (256, 256), 0)
            hot = jnp.where(source == index_ref[kind, side : side + 1, :], 1.0, 0.0)
            table_ref[kind, side * 256 : side * 256 + 256, :] = hot.astype(BF16)
    all_ref[0:16] = first_ref[...]
    all_ref[16:32] = second_ref[...]
    all_ref[32:48] = jnp.broadcast_to(loss_ref[...], (16, 4096))
    for a in range(N):
        m = (N - a) % N
        x = jnp.concatenate(
            [all_ref[:, a * 256 : a * 256 + 256], all_ref[:, m * 256 : m * 256 + 256]], axis=1
        )
        high = x.astype(BF16)
        rest = x - high.astype(F32)
        mid = rest.astype(BF16)
        low = (rest - mid.astype(F32)).astype(BF16)
        parts = jnp.concatenate([high, mid, low], axis=0)
        o = lax.dot_general(parts, table_ref[kind_of(a)], NN, preferred_element_type=F32)
        mid_ref[a] = 0.5 * (o[0:48] + o[48:96] + o[96:144])
    for row in range(N):
        tile = slice(row // 8 * 128, row // 8 * 128 + 128)
        lane = lax.broadcasted_iota(jnp.int32, (48, 128), 1) // 16
        for half in range(2):
            total = jnp.zeros((48, 128), F32)
            for s in range(8):
                v = mid_ref[8 * half + s, :, tile]
                shift = (s - row) % 8 * 16
                v = pltpu.roll(v, shift, 1) if shift else v
                total = jnp.where(lane == s, v, total)
            out_ref[row, :, 128 * half : 128 * half + 128] = total


def pack_kernels(first, second, loss, table):
    return pl.pallas_call(
        pack_body,
        out_shape=jax.ShapeDtypeStruct((N, 48, 256), F32),
        scratch_shapes=[
            pltpu.VMEM((48, 4096), F32),
            pltpu.VMEM((N, 48, 256), F32),
            pltpu.VMEM((4, 512, 256), BF16),
        ],
        cost_estimate=pl.CostEstimate(flops=1 << 30, bytes_accessed=3 << 20, transcendentals=0),
        name="pack",
    )(first, second, loss.reshape(1, 4096), table)


def spectrum(load, jt_ref, kt_ref, x1_ref, x2_ref, sr_ref, s_ref, fr, fi):
    def rows(t, _):
        r = pl.ds(pl.multiple_of(t * 16, 16), 16)
        for half in range(2):
            x = [load(i, r, half).astype(BF16).astype(F32) for i in range(N)]
            even = [x[0]] + [x[n] + x[N - n] for n in range(1, 8)]
            odd = [None] + [x[n] - x[N - n] for n in range(1, 8)]
            lanes = slice(half * 128, half * 128 + 128)
            for a in range(9):
                re = even[0] + x[8] if a % 2 == 0 else even[0] - x[8]
                im = None
                for n in range(1, 8):
                    c, s = float(fr[a, n]), float(fi[a, n])
                    if abs(c) > 1e-6:
                        re = re + (even[n] * c if abs(c) < 1 else even[n] if c > 0 else -even[n])
                    if abs(s) > 1e-6:
                        term = odd[n] * s
                        im = term if im is None else im + term
                x1_ref[a, r, lanes] = re.astype(BF16)
                im = jnp.zeros_like(re) if im is None else im
                x1_ref[a, r, half * 128 + 256 : half * 128 + 384] = im.astype(BF16)
        return 0

    lax.fori_loop(0, 8, rows, 0)
    for a in range(9):
        o = lax.dot_general(jt_ref[...], x1_ref[a], NT, preferred_element_type=F32)
        x2_ref[a] = o.astype(BF16)
    for a in range(N):
        src = a if a <= 8 else N - a
        o = lax.dot_general(kt_ref[kind_of(a)], x2_ref[src], NN, preferred_element_type=F32)
        sr_ref[:, a * 16 : a * 16 + 16, :] = o.astype(BF16).reshape(N, 16, 128)
    for row in range(N):
        s_ref[row] = sr_ref[row].astype(F32).T


def collide_body(
    fr, fi, x_ref, fluid_ref, k_ref, jt_ref, kt_ref, ib_ref, ia_ref, out_ref,
    x1_ref, x2_ref, sr_ref, s_ref, z_ref, g_ref,
):
    def load(i, r, half):
        at = (i % 2) * 256 + half * 128
        return x_ref[i // 2, r, at : at + 128]

    spectrum(load, jt_ref, kt_ref, x1_ref, x2_ref, sr_ref, s_ref, fr, fi)
    g_ref[...] = jnp.zeros_like(g_ref)

    def direction(p, _):
        for row in range(N):
            s = s_ref[row]
            one = s * k_ref[row, pl.ds(p, 1), :]
            two = s * k_ref[row, pl.ds(16 + p, 1), :]
            both = jnp.concatenate([one.astype(BF16), two.astype(BF16)], axis=0)
            kind = 1 if row % 8 == 0 else 0
            o = lax.dot_general(ib_ref[kind], both, NT, preferred_element_type=F32)
            z_ref[:, row * 16 : row * 16 + 16, :] = o.astype(BF16).reshape(N, 16, 256)
        for i in range(N):
            o = lax.dot_general(ia_ref[...], z_ref[i], NN, preferred_element_type=F32)
            g_ref[i] += o[:, :128] * o[:, 128:]
        return 0

    lax.fori_loop(0, DIRS, direction, 0)
    for row in range(N):
        one = (s_ref[row] * k_ref[row, 32:33, :]).astype(BF16)
        kind = 1 if row % 8 == 0 else 0
        o = lax.dot_general(ib_ref[kind], one, NT, preferred_element_type=F32)
        z_ref[:, row * 16 : row * 16 + 16, :128] = o.astype(BF16).reshape(N, 16, 128)
    fluid = fluid_ref[...] == 0
    for i in range(N):
        loss = lax.dot_general(ia_ref[...], z_ref[i, :, :128], NN, preferred_element_type=F32)
        lanes = slice((i % 2) * 256, (i % 2) * 256 + 256)
        x = x_ref[i // 2, :, lanes]
        change = g_ref[i].T - x * loss.T
        out_ref[i // 2, :, lanes] = jnp.where(fluid, x + collision_timestep * change, x)


def constant_tables():
    fr, fi, ir, ii = line_tables()
    to = lambda t: np.asarray(t, np.float32).astype(BF16)
    return (fr, fi), tuple(
        to(t) for t in (j_table(fr, fi), k_tables(fr, fi), inverse_i_tables(ir, ii), inverse_jk_table(ir, ii))
    ), packing_index()


def collide(x, cells, packed, lines, tables):
    return pl.pallas_call(
        functools.partial(collide_body, *lines),
        out_shape=jax.ShapeDtypeStruct((8, 128, 512), F32),
        scratch_shapes=[
            pltpu.VMEM((9, 128, 512), BF16),
            pltpu.VMEM((9, 512, 128), BF16),
            pltpu.VMEM((N, 256, 128), BF16),
            pltpu.VMEM((N, 128, 256), F32),
            pltpu.VMEM((N, 256, 256), BF16),
            pltpu.VMEM((N, 256, 128), F32),
        ],
        compiler_params=pltpu.CompilerParams(vmem_limit_bytes=40 << 20),
        cost_estimate=pl.CostEstimate(flops=18 << 30, bytes_accessed=8 << 20, transcendentals=0),
        name="collide",
    )(x, cells, packed, *tables)


def components(nvel):
    levels = (2.0 * jnp.arange(nvel, dtype=F32) - (nvel - 1)) / (nvel - 1)
    along_x = jnp.repeat(levels, nvel * nvel)
    along_y = jnp.tile(jnp.repeat(levels, nvel), nvel)
    along_z = jnp.tile(levels, nvel * nvel)
    return along_x, along_y, along_z


def wall_tables(along_x, along_y, along_z):
    still_wall = jnp.exp(-4.5 * (along_x * along_x + along_y * along_y + along_z * along_z))
    still_wall = still_wall / jnp.sum(still_wall)
    moving = jnp.exp(
        -0.5 * ((3.0 * along_x - 1.0) ** 2 + 9.0 * along_y * along_y + 9.0 * along_z * along_z)
    )
    moving = moving / jnp.sum(moving)
    return still_wall, moving


def transport(padded, along_x, along_y):
    center = padded[1:-1, 1:-1]
    back_x = center - padded[:-2, 1:-1]
    front_x = padded[2:, 1:-1] - center
    back_y = center - padded[1:-1, :-2]
    front_y = padded[1:-1, 2:] - center
    plus_x = jnp.maximum(along_x, 0.0)[None, None, :]
    minus_x = jnp.minimum(along_x, 0.0)[None, None, :]
    plus_y = jnp.maximum(along_y, 0.0)[None, None, :]
    minus_y = jnp.minimum(along_y, 0.0)[None, None, :]
    return -courant * (plus_x * back_x + minus_x * front_x + plus_y * back_y + minus_y * front_y)


def on_device(lines, tables, one_hot, distribution, cell_type, first, second, loss):
    rows, cols, block = distribution.shape
    groups = lax.axis_size("vel")
    rank = lax.axis_index("vel")
    slab = rows // groups
    along_x, along_y, along_z = components(N)
    still, moving = wall_tables(along_x, along_y, along_z)
    here = lambda t: lax.dynamic_slice_in_dim(t, rank * block, block)
    partial = jnp.sum(distribution, axis=2)
    copies = lax.all_to_all(
        jnp.broadcast_to(partial[None], (groups, rows, cols)), "vel", 0, 0, tiled=True
    )
    density = jnp.sum(copies, axis=0)
    fluid = (cell_type == 0)[:, :, None]
    wall = jnp.where(cell_type[:, :, None] == 1, here(still)[None, None, :], here(moving)[None, None, :])
    walled = jnp.where(fluid, distribution, density[:, :, None] * wall)
    count = lax.axis_size("cell")
    up = [(i, i + 1) for i in range(count - 1)]
    below = lax.ppermute(walled[:, cols - 1 :], "cell", up)
    above = lax.ppermute(walled[:, :1], "cell", [(b, a) for a, b in up])
    rimmed = jnp.concatenate([below, walled, above], axis=1)
    padded = jnp.pad(rimmed, ((1, 1), (0, 0), (0, 0)))
    moved = jnp.where(fluid, walled + transport(padded, here(along_x), here(along_y)), walled)
    sent = lax.all_to_all(moved.reshape(groups, slab, cols, block), "vel", 0, 0, tiled=True)
    packed = pack_kernels(first, second, loss, one_hot)
    types = lax.dynamic_slice_in_dim(cell_type, rank * slab, slab, 0).reshape(slab * cols, 1)
    done = collide(sent.reshape(groups, slab * cols, block), types, packed, lines, tables)
    back = lax.all_to_all(done.reshape(groups, slab, cols, block), "vel", 0, 0, tiled=True)
    return back.reshape(rows, cols, block)


def solution(mesh):
    lines, tables, one_hot = constant_tables()

    def body(*arguments):
        return on_device(lines, tables, jnp.asarray(one_hot), *arguments)

    return jax.shard_map(
        body,
        mesh=mesh,
        in_specs=(P(None, "cell", "vel"), P(None, "cell"), P(), P(), P()),
        out_specs=P(None, "cell", "vel"),
        check_vma=False,
    )
```

time: 604 us -> 129 us (0.21); the launches traced: 597 us -> 129 us
  matrix products: 343 us -> 0 us
  local copies, waits for them, and re-layouts: 142 us -> 8.32 us
  Pallas kernels: 0 us -> 31.5 us
  blocking collectives: 17.7 us -> 33.4 us
  waiting for transfers between devices: 46.2 us -> 31.1 us
  loops' own time: 14.1 us -> 0 us
  starting transfers between devices: 23.6 us -> 17.3 us
    dot_general x340 -> x0, matrix products: 343 us -> none  [apply_table(): jnp.einsum(pattern, matrix, operand, preferred_element_type=jnp.float32)]
    while x64 -> x0, local copies, waits for them, and re-layouts: 39.2 us -> none
    reshape x5 -> x2, local copies, waits for them, and re-layouts: 37.6 us -> 2.59 us  [the longest x1 2.51 us: on_device(): moved.reshape(groups, slab, cols, block)]
    pallas_call x0 -> x2, Pallas kernels: none -> 31.5 us  [the longest x1 27.6 us: collide(): pl.pallas_call(functools.partial(collide_body, *lines), out_shape=jax.Sha...]
    mul x3 -> x0, local copies, waits for them, and re-layouts: 29.1 us -> none  [the longest x2 29.1 us: on_device(): collision_timestep * collision_operator]
    dynamic_slice x48 -> x2, local copies, waits for them, and re-layouts: 19.5 us -> 0.15 us  [on_device(): lax.dynamic_slice_in_dim(cell_type, rank * slab, slab, 0)]
    all_to_all x1, blocking collectives: 17.7 us -> 33.4 us  [on_device(): lax.all_to_all(done.reshape(groups, slab, cols, block), 'vel', 0, 0, tile...]
    all_to_all x3 -> x2, waiting for transfers between devices: 39 us -> 23.8 us  [the longest x1 21.4 us: on_device(): lax.all_to_all(moved.reshape(groups, slab, cols, block), 'vel', 0, 0, til...]
  transfers between devices with their start and end apart: 5 -> 4, of which waited for: 5 -> 4; matrix products, arithmetic and copies ran while one was open for 1% -> 2% of each run, Pallas kernels for 0% -> 3%
where the time goes in v1:
time: 129 us
  blocking collectives  33.4 us (26%)
  Pallas kernels  31.5 us (24%)
  waiting for transfers between devices  31.1 us (24%)
  starting transfers between devices  17.3 us (13%)
  local copies, waits for them, and re-layouts  8.32 us (6%)
  other arithmetic  7.23 us (6%)
    all_to_all x1, blocking collectives, on_device(): lax.all_to_all(done.reshape(groups, slab, cols, block), 'vel', 0, 0, tile...  33.4 us
    pallas_call x1, Pallas kernels, collide(): pl.pallas_call(functools.partial(collide_body, *lines), out_shape=jax.Sha...  27.6 us
    all_to_all x1, waiting for transfers between devices, on_device(): lax.all_to_all(moved.reshape(groups, slab, cols, block), 'vel', 0, 0, til...  21.4 us
    ppermute x1, starting transfers between devices, on_device(): below = lax.ppermute(walled[:, cols - 1:], 'cell', up)  6.52 us
    ppermute x1, waiting for transfers between devices, on_device(): above = lax.ppermute(walled[:, :1], 'cell', [(b, a) for a, b in up])  5.9 us
    all_to_all x1, starting transfers between devices, on_device(): lax.all_to_all(jnp.broadcast_to(partial[None], (groups, rows, cols)), 've...  5.03 us
    unnamed x19, local copies, waits for them, and re-layouts  4.51 us
    pallas_call x1, Pallas kernels, pack_kernels(): pl.pallas_call(pack_body, out_shape=jax.ShapeDtypeStruct((N, 48, 256), F3...  3.94 us
  transfers between devices with their start and end apart: 4, of which 4 were waited for; matrix products, arithmetic and copies ran while one was open for 2% of the time, Pallas kernels for 3%

profile of v1, /device:TPU:33, one launch (start us, length us, event | category | flops | bytes accessed | tf_op | source)
XLA Modules:
  0.0 129.0 jit_solution(17848664837478449521)
XLA Ops:
  0.0 0.0 copy-start.5
  0.0 0.0 copy-start.6
  0.0 2.0 %reduce_sum.36 = f32[128,8]{1,0:T(8,128)S(1)} reduce(f32[128,8,512]{2,1,0:T(8,128)} %param.10, f32[]{:T(128)} %constant.11.clone.1), dimensions={2}, to_apply=%region_0.0 | reduce | flops 523264 | bytes 2101252 | tf_op jit(solution)/shard_map/reduce_sum | solution.py:306
  2.0 0.6 broadcast_in_dim.73
  2.7 5.0 %all-to-all-start = ((f32[8,128,8]{1,2,0:T(8,128)}), f32[8,128,8]{1,2,0:T(8,128)S(1)}, u32[]{:S(2)}, u32[]{:S(2)}) async-start(f32[8,128,8]{1,2,0:T(8,128)} %broadcast_in_dim.73), calls=%async_computation | async-start | bytes 65536 | tf_op jit(solution)/shard_map/all_to_all | solution.py:307
  7.7 0.1 broadcast_in_dim.76
  7.8 0.1 tile.55
  7.9 0.1 broadcast_bitcast_fusion.1
  8.0 0.1 tile.62
  8.1 0.1 tile.59
  8.2 0.0 copy-done.6
  8.3 0.8 exponential_reduce_fusion
  9.0 1.4 %dynamic-slice_maximum_fusion = (f32[512]{0:T(512)S(1)}, f32[512]{0:T(512)S(1)}, f32[512]{0:T(512)S(1)}, f32[512]{0:T(512)S(1)}, f32[512]{0:T(512)S(1)}, /*index=5*/f32[512]{0:T(512)S(1)}) fusion(f32[4096]{0:T(1024)S(1)} %bitcast.18, s32[]{:T(128)S(6)} %select_n.20, f32[]{:T(128)} %get-tuple-element.21, f32[4096]{0:T(1024)S(1)} %tile.59, ...), kind=kLoop, calls=%fused_computation.41 | loop fusion | flops 9728 | bytes 22540 | tf_op jit(solution)/shard_map/max | solution.py:291
  10.4 2.4 %all-to-all-done = f32[8,128,8]{1,2,0:T(8,128)S(1)} async-done(((f32[8,128,8]{1,2,0:T(8,128)}), f32[8,128,8]{1,2,0:T(8,128)S(1)}, u32[]{:S(2)}, u32[]{:S(2)}) %all-to-all-start) | async-done | bytes 32800 | tf_op jit(solution)/shard_map/all_to_all | solution.py:307
  12.8 0.0 copy-done.5
  12.8 1.3 %copy_select_fusion = f32[128,8,512]{2,0,1:T(8,128)S(1)} fusion(f32[128,8,512]{2,1,0:T(8,128)S(1)} %copy-done.5, f32[512]{0:T(512)S(1)} %get-tuple-element.11, f32[512]{0:T(512)S(1)} %get-tuple-element.12, f32[128,8]{0,1:T(8,128)S(1)} %reduce_sum.37, pred[128,8]{0,1:T(8,128)(4,1)S(1)} %get-tuple-element.16, pred[128,8]{0,1:T(8,128)(4,1)S(1)} %get-tuple-element.15), kind=kLoop, calls=%fused_computation.20 | loop fusion | flops 1572864 | bytes 4204544 | tf_op jit(solution)/shard_map/jit(_where)/select_n | solution.py:313
  14.2 6.5 %collective-permute-start = (f32[128,1,512]{2,0,1:T(8,128)S(1)}, f32[128,1,512]{2,0,1:T(8,128)S(1)}, u32[]{:S(2)}, u32[]{:S(2)}) collective-permute-start(f32[128,1,512]{2,0,1:T(8,128)S(1)} %get-tuple-element.5), channel_id=1, source_target_pairs={{0,8},{8,16},{16,24},{24,32},{32,40},{40,48},{48,56},{56,64},{64,7... | collective-permute-start | bytes 786440 | tf_op jit(solution)/shard_map/ppermute | solution.py:316
  20.7 1.9 %collective-permute-start.1 = (f32[128,1,512]{2,0,1:T(8,128)S(1)}, f32[128,1,512]{2,0,1:T(8,128)S(1)}, u32[]{:S(2)}, u32[]{:S(2)}) collective-permute-start(f32[128,1,512]{2,0,1:T(8,128)S(1)} %get-tuple-element.6), channel_id=1, source_target_pairs={{8,0},{16,8},{24,16},{32,24},{40,32},{48,40},{56,48},{64,56},{72,6... | collective-permute-start | bytes 786440 | tf_op jit(solution)/shard_map/ppermute | solution.py:317
  22.7 1.4 %collective-permute-done = f32[128,1,512]{2,0,1:T(8,128)S(1)} collective-permute-done((f32[128,1,512]{2,0,1:T(8,128)S(1)}, f32[128,1,512]{2,0,1:T(8,128)S(1)}, u32[]{:S(2)}, u32[]{:S(2)}) %collective-permute-start) | collective-permute-done | bytes 262176 | tf_op jit(solution)/shard_map/ppermute | solution.py:316
  24.0 5.9 %collective-permute-done.1 = f32[128,1,512]{2,0,1:T(8,128)S(1)} collective-permute-done((f32[128,1,512]{2,0,1:T(8,128)S(1)}, f32[128,1,512]{2,0,1:T(8,128)S(1)}, u32[]{:S(2)}, u32[]{:S(2)}) %collective-permute-start.1) | collective-permute-done | bytes 262176 | tf_op jit(solution)/shard_map/ppermute | solution.py:317
  29.9 0.5 select_maximum_fusion
  30.4 1.2 add_select_fusion
  31.7 2.5 %copy.30 = f32[8,16,8,512]{3,2,1,0:T(8,128)} copy(f32[8,16,8,512]{3,1,0,2:T(8,128)S(1)} %bitcast.14) | data formatting | bytes 4194304 | tf_op jit(solution)/shard_map/reshape | solution.py:321
  34.2 3.8 %all-to-all-start.1 = ((f32[8,16,8,512]{3,2,1,0:T(8,128)}), f32[8,16,8,512]{3,2,1,0:T(8,128)S(1)}, u32[]{:S(2)}, u32[]{:S(2)}) async-start(f32[8,16,8,512]{3,2,1,0:T(8,128)} %copy.30), calls=%async_computation.1 | async-start | bytes 4194304 | tf_op jit(solution)/shard_map/all_to_all | solution.py:321
  38.0 0.0 copy-start
  38.0 0.0 copy-start.2
  38.0 0.1 constant_dynamic-slice_fusion
  38.1 0.1 copy.31
  38.2 0.1 reshape.54.fluid_ref
  38.2 3.9 %pack.1.k_ref = f32[16,48,256]{2,1,0:T(8,128)} custom-call(f32[16,4096]{1,0:T(8,128)} %first_ref.1, f32[16,4096]{1,0:T(8,128)} %second_ref.1, f32[1,4096]{1,0:T(1,128)} %bitcast.19, s32[4,2,256]{2,1,0:T(2,128)} %constant.53.clone.index_ref), custom_call_target="tpu_custom_call" | custom-call | flops 1073741824 | bytes 3145728 | tf_op jit(solution)/shard_map/pack/pallas_call | solution.py:153
  42.2 21.4 %all-to-all-done.1 = f32[8,16,8,512]{3,2,1,0:T(8,128)S(1)} async-done(((f32[8,16,8,512]{3,2,1,0:T(8,128)}), f32[8,16,8,512]{3,2,1,0:T(8,128)S(1)}, u32[]{:S(2)}, u32[]{:S(2)}) %all-to-all-start.1) | async-done | bytes 2097184 | tf_op jit(solution)/shard_map/all_to_all | solution.py:321
  63.6 0.0 copy-done
  63.6 0.0 copy-done.2
  63.6 0.0 copy-start.1
  63.6 1.0 copy-done.1
  64.7 0.0 copy-start.3
  64.7 0.9 copy-done.3
  65.6 0.0 copy-start.4
  65.6 1.1 copy-done.4
  66.7 27.6 %collide.1 = f32[8,128,512]{2,1,0:T(8,128)S(1)} custom-call(f32[8,128,512]{2,1,0:T(8,128)S(1)} %bitcast.11, s32[128,1]{1,0:T(8,128)S(1)} %reshape.54.fluid_ref, f32[16,48,256]{2,1,0:T(8,128)S(1)} %copy-done.4, bf16[512,512]{1,0:T(8,128)(2,1)S(1)} %copy-done.1, bf16[4,256,512]{2,1,0:T(8,128)(2,1)S(1)} %copy-done, bf16[2,256,256]{2,1,0:T(8,128)(2,1)S(1)} %copy-done.2, ...), custom_call_target="tpu_custom_call" | custom-call | flops 19327352832 | bytes 8388608 | tf_op jit(solution)/shard_map/collide/pallas_call | solution.py:250
  94.3 33.4 %all_to_all.15 = f32[8,16,8,512]{3,2,1,0:T(8,128)S(1)} all-to-all(f32[8,16,8,512]{3,2,1,0:T(8,128)S(1)} %bitcast.12), channel_id=1, replica_groups=mesh['cell'=16,'vel'=8] {'vel'}, dimensions={0} | all-to-all | bytes 4194304 | tf_op jit(solution)/shard_map/all_to_all | solution.py:325
  127.6 1.3 %copy.37 = f32[128,8,512]{2,1,0:T(8,128)} copy(f32[128,8,512]{2,1,0:T(8,128)S(1)} %bitcast.13) | data formatting | bytes 4194304
  (15 shorter events, 0.2 us)
Async XLA Ops:
  0.0 12.8 %copy-start.5 = (f32[128,8,512]{2,1,0:T(8,128)S(1)}, f32[128,8,512]{2,1,0:T(8,128)}, u32[]{:S(2)}) copy-start(f32[128,8,512]{2,1,0:T(8,128)} %param.10) | copy-start | bytes 6291460
  0.0 8.2 %copy-start.6 = (s32[128,8]{0,1:T(8,128)S(1)}, s32[128,8]{0,1:T(8,128)}, u32[]{:S(2)}) copy-start(s32[128,8]{0,1:T(8,128)} %param.11) | copy-start | bytes 12292
  2.7 10.1 %all-to-all-start = ((f32[8,128,8]{1,2,0:T(8,128)}), f32[8,128,8]{1,2,0:T(8,128)S(1)}, u32[]{:S(2)}, u32[]{:S(2)}) async-start(f32[8,128,8]{1,2,0:T(8,128)} %broadcast_in_dim.73), calls=%async_computation | async-start | bytes 65536 | tf_op jit(solution)/shard_map/all_to_all | solution.py:307
  14.2 9.8 %collective-permute-start = (f32[128,1,512]{2,0,1:T(8,128)S(1)}, f32[128,1,512]{2,0,1:T(8,128)S(1)}, u32[]{:S(2)}, u32[]{:S(2)}) collective-permute-start(f32[128,1,512]{2,0,1:T(8,128)S(1)} %get-tuple-element.5), channel_id=1, source_target_pairs={{0,8},{8,16},{16,24},{24,32},{32,40},{40,48},{48,56},{56,64},{64,7... | collective-permute-start | bytes 786440 | tf_op jit(solution)/shard_map/ppermute | solution.py:316
  20.7 9.2 %collective-permute-start.1 = (f32[128,1,512]{2,0,1:T(8,128)S(1)}, f32[128,1,512]{2,0,1:T(8,128)S(1)}, u32[]{:S(2)}, u32[]{:S(2)}) collective-permute-start(f32[128,1,512]{2,0,1:T(8,128)S(1)} %get-tuple-element.6), channel_id=1, source_target_pairs={{8,0},{16,8},{24,16},{32,24},{40,32},{48,40},{56,48},{64,56},{72,6... | collective-permute-start | bytes 786440 | tf_op jit(solution)/shard_map/ppermute | solution.py:317
  34.2 29.4 %all-to-all-start.1 = ((f32[8,16,8,512]{3,2,1,0:T(8,128)}), f32[8,16,8,512]{3,2,1,0:T(8,128)S(1)}, u32[]{:S(2)}, u32[]{:S(2)}) async-start(f32[8,16,8,512]{3,2,1,0:T(8,128)} %copy.30), calls=%async_computation.1 | async-start | bytes 4194304 | tf_op jit(solution)/shard_map/all_to_all | solution.py:321
  38.0 25.7 %copy-start = (bf16[4,256,512]{2,1,0:T(8,128)(2,1)S(1)}, bf16[4,256,512]{2,1,0:T(8,128)(2,1)}, u32[]{:S(2)}) copy-start(bf16[4,256,512]{2,1,0:T(8,128)(2,1)} %constant.55.clone.kt_ref) | copy-start | bytes 3145732
  38.0 25.6 %copy-start.2 = (bf16[2,256,256]{2,1,0:T(8,128)(2,1)S(1)}, bf16[2,256,256]{2,1,0:T(8,128)(2,1)}, u32[]{:S(2)}) copy-start(bf16[2,256,256]{2,1,0:T(8,128)(2,1)} %constant.56.clone.ib_ref) | copy-start | bytes 786436
  63.6 1.0 copy-start.1
  64.7 0.9 copy-start.3
  65.6 1.1 copy-start.4

commit v2 on v1

--- a/solution.py
+++ b/solution.py
@@ -115,15 +115,12 @@
     return 0 if a == 0 else 1 if a < 8 else 2 if a == 8 else 3
 
 
-def pack_body(first_ref, second_ref, loss_ref, index_ref, out_ref, all_ref, mid_ref, table_ref):
+def pack(index_ref, all_ref, mid_ref, hot_ref, k_ref):
     for kind in range(4):
         for side in range(2):
             source = lax.broadcasted_iota(jnp.int32, (256, 256), 0)
             hot = jnp.where(source == index_ref[kind, side : side + 1, :], 1.0, 0.0)
-            table_ref[kind, side * 256 : side * 256 + 256, :] = hot.astype(BF16)
-    all_ref[0:16] = first_ref[...]
-    all_ref[16:32] = second_ref[...]
-    all_ref[32:48] = jnp.broadcast_to(loss_ref[...], (16, 4096))
+            hot_ref[kind, side * 256 : side * 256 + 256, :] = hot.astype(BF16)
     for a in range(N):
         m = (N - a) % N
         x = jnp.concatenate(
@@ -134,11 +131,11 @@
         mid = rest.astype(BF16)
         low = (rest - mid.astype(F32)).astype(BF16)
         parts = jnp.concatenate([high, mid, low], axis=0)
-        o = lax.dot_general(parts, table_ref[kind_of(a)], NN, preferred_element_type=F32)
+        o = lax.dot_general(parts, hot_ref[kind_of(a)], NN, preferred_element_type=F32)
         mid_ref[a] = 0.5 * (o[0:48] + o[48:96] + o[96:144])
+    lane = lax.broadcasted_iota(jnp.int32, (48, 128), 1) // 16
     for row in range(N):
         tile = slice(row // 8 * 128, row // 8 * 128 + 128)
-        lane = lax.broadcasted_iota(jnp.int32, (48, 128), 1) // 16
         for half in range(2):
             total = jnp.zeros((48, 128), F32)
             for s in range(8):
@@ -146,24 +143,13 @@
                 shift = (s - row) % 8 * 16
                 v = pltpu.roll(v, shift, 1) if shift else v
                 total = jnp.where(lane == s, v, total)
-            out_ref[row, :, 128 * half : 128 * half + 128] = total
-
-
-def pack_kernels(first, second, loss, table):
-    return pl.pallas_call(
-        pack_body,
-        out_shape=jax.ShapeDtypeStruct((N, 48, 256), F32),
-        scratch_shapes=[
-            pltpu.VMEM((48, 4096), F32),
-            pltpu.VMEM((N, 48, 256), F32),
-            pltpu.VMEM((4, 512, 256), BF16),
-        ],
-        cost_estimate=pl.CostEstimate(flops=1 << 30, bytes_accessed=3 << 20, transcendentals=0),
-        name="pack",
-    )(first, second, loss.reshape(1, 4096), table)
-
-
-def spectrum(load, jt_ref, kt_ref, x1_ref, x2_ref, sr_ref, s_ref, fr, fi):
+            k_ref[row, :, 128 * half : 128 * half + 128] = total
+
+
+ORDER = (1, 2, 3, 4, 5, 6, 7, 8, 0)
+
+
+def spectrum(fr, fi, load, jt_ref, kt_ref, x1_ref, x2_ref, sr_ref, s_ref):
     def rows(t, _):
         r = pl.ds(pl.multiple_of(t * 16, 16), 16)
         for half in range(2):
@@ -171,7 +157,7 @@
             even = [x[0]] + [x[n] + x[N - n] for n in range(1, 8)]
             odd = [None] + [x[n] - x[N - n] for n in range(1, 8)]
             lanes = slice(half * 128, half * 128 + 128)
-            for a in range(9):
+            for place, a in enumerate(ORDER):
                 re = even[0] + x[8] if a % 2 == 0 else even[0] - x[8]
                 im = None
                 for n in range(1, 8):
@@ -181,87 +167,229 @@
                     if abs(s) > 1e-6:
                         term = odd[n] * s
                         im = term if im is None else im + term
-                x1_ref[a, r, lanes] = re.astype(BF16)
                 im = jnp.zeros_like(re) if im is None else im
-                x1_ref[a, r, half * 128 + 256 : half * 128 + 384] = im.astype(BF16)
+                at = pl.ds(pl.multiple_of(place * CELLS + t * 16, 16), 16)
+                x1_ref[at, lanes] = re.astype(BF16)
+                x1_ref[at, half * 128 + 256 : half * 128 + 384] = im.astype(BF16)
         return 0
 
-    lax.fori_loop(0, 8, rows, 0)
-    for a in range(9):
-        o = lax.dot_general(jt_ref[...], x1_ref[a], NT, preferred_element_type=F32)
-        x2_ref[a] = o.astype(BF16)
-    for a in range(N):
-        src = a if a <= 8 else N - a
-        o = lax.dot_general(kt_ref[kind_of(a)], x2_ref[src], NN, preferred_element_type=F32)
-        sr_ref[:, a * 16 : a * 16 + 16, :] = o.astype(BF16).reshape(N, 16, 128)
+    lax.fori_loop(0, CELLS // 16, rows, 0)
+    wide = 4 * CELLS
+    for first, size in ((0, wide), (wide, wide), (2 * wide, CELLS)):
+        part = x1_ref[first : first + size, :]
+        o = lax.dot_general(jt_ref[...], part, NT, preferred_element_type=F32)
+        x2_ref[:, first : first + size] = o.astype(BF16)
+
+    def put(kind, first, size, places):
+        o = lax.dot_general(
+            kt_ref[kind], x2_ref[:, first : first + size], NN, preferred_element_type=F32
+        )
+        for t, a in enumerate(places):
+            v = o[:, t * CELLS : t * CELLS + CELLS].astype(BF16)
+            sr_ref[:, a * 16 : a * 16 + 16, :] = v.reshape(N, 16, CELLS)
+
+    put(1, 0, wide, (1, 2, 3, 4))
+    put(3, 0, wide, (15, 14, 13, 12))
+    put(1, wide, wide, (5, 6, 7))
+    put(3, wide, wide, (11, 10, 9))
+    put(2, wide + 3 * CELLS, CELLS, (8,))
+    put(0, 2 * wide, CELLS, (0,))
     for row in range(N):
         s_ref[row] = sr_ref[row].astype(F32).T
 
 
-def collide_body(
-    fr, fi, x_ref, fluid_ref, k_ref, jt_ref, kt_ref, ib_ref, ia_ref, out_ref,
+CHUNKS = 2
+CELLS = 128 // CHUNKS
+GROUP = 8
+
+
+def remote(src, dst, send, recv, peer):
+    return pltpu.make_async_remote_copy(
+        src_ref=src,
+        dst_ref=dst,
+        send_sem=send,
+        recv_sem=recv,
+        device_id={"vel": peer},
+        device_id_type=pl.DeviceIdType.MESH,
+    )
+
+
+def step_body(
+    fr, fi, moved_ref, fluid_ref, index_ref, first_ref, second_ref, loss_ref,
+    jt_hbm, kt_hbm, ib_hbm, ia_hbm, out_ref,
+    x_ref, r_ref, all_ref, mid_ref, hot_ref, k_ref, jt_ref, kt_ref, ib_ref, ia_ref,
     x1_ref, x2_ref, sr_ref, s_ref, z_ref, g_ref,
+    send_sem, recv_sem, back_send, back_recv, own_sem, load_sem,
 ):
-    def load(i, r, half):
-        at = (i % 2) * 256 + half * 128
-        return x_ref[i // 2, r, at : at + 128]
-
-    spectrum(load, jt_ref, kt_ref, x1_ref, x2_ref, sr_ref, s_ref, fr, fi)
-    g_ref[...] = jnp.zeros_like(g_ref)
-
-    def direction(p, _):
+    me = lax.axis_index("vel")
+    barrier = pltpu.get_barrier_semaphore()
+    for s in range(1, GROUP):
+        pl.semaphore_signal(
+            barrier, inc=1, device_id={"vel": lax.rem(me + s, GROUP)},
+            device_id_type=pl.DeviceIdType.MESH,
+        )
+    loads = [
+        pltpu.make_async_copy(first_ref, all_ref.at[0:16], load_sem.at[0]),
+        pltpu.make_async_copy(second_ref, all_ref.at[16:32], load_sem.at[1]),
+        pltpu.make_async_copy(loss_ref, all_ref.at[32:40], load_sem.at[2]),
+    ]
+    tables = [
+        pltpu.make_async_copy(jt_hbm, jt_ref, load_sem.at[3]),
+        pltpu.make_async_copy(kt_hbm, kt_ref, load_sem.at[4]),
+        pltpu.make_async_copy(ib_hbm, ib_ref, load_sem.at[5]),
+        pltpu.make_async_copy(ia_hbm, ia_ref, load_sem.at[6]),
+    ]
+    own = [
+        pltpu.make_async_copy(moved_ref.at[me, c], x_ref.at[c, me], own_sem.at[c])
+        for c in range(CHUNKS)
+    ]
+    for copy in loads + tables + own:
+        copy.start()
+    pl.semaphore_wait(barrier, GROUP - 1)
+
+    def send(c, s):
+        peer = lax.rem(me + s, GROUP)
+        return remote(
+            moved_ref.at[peer, c], x_ref.at[c, me], send_sem.at[c, s], recv_sem.at[c, s], peer
+        )
+
+    def start(c):
+        for s in range(1, GROUP):
+            send(c, s).start()
+
+    start(0)
+    for copy in loads:
+        copy.wait()
+    all_ref[40:48] = jnp.zeros((8, 4096), F32)
+    pack(index_ref, all_ref, mid_ref, hot_ref, k_ref)
+    for copy in tables + own:
+        copy.wait()
+    for s in range(1, GROUP):
+        send(0, s).wait_send()
+    start(1)
+
+    def chunk(c, _):
+        for s in range(1, GROUP):
+            send(c, s).wait_recv()
+
+        def load(i, r, half):
+            at = (i % 2) * 256 + half * 128
+            return x_ref[c, i // 2, r, at : at + 128]
+
+        spectrum(fr, fi, load, jt_ref, kt_ref, x1_ref, x2_ref, sr_ref, s_ref)
+        g_ref[...] = jnp.zeros_like(g_ref)
+
+        def directions(q, _):
+            for row in range(N):
+                s = s_ref[row]
+                both = [
+                    (s * k_ref[row, pl.ds(base + CHUNKS * q + t, 1), :]).astype(BF16)
+                    for base in (0, 16)
+                    for t in range(CHUNKS)
+                ]
+                kind = 1 if row % 8 == 0 else 0
+                o = lax.dot_general(
+                    ib_ref[kind], jnp.concatenate(both, axis=0), NT, preferred_element_type=F32
+                )
+                z_ref[:, row * 16 : row * 16 + 16, :] = o.astype(BF16).reshape(N, 16, 256)
+            for i in range(N):
+                o = lax.dot_general(ia_ref[...], z_ref[i], NN, preferred_element_type=F32)
+                g_ref[i] += o[:, :128] * o[:, 128:]
+            return 0
+
+        lax.fori_loop(0, DIRS // CHUNKS, directions, 0)
         for row in range(N):
-            s = s_ref[row]
-            one = s * k_ref[row, pl.ds(p, 1), :]
-            two = s * k_ref[row, pl.ds(16 + p, 1), :]
-            both = jnp.concatenate([one.astype(BF16), two.astype(BF16)], axis=0)
+            one = (s_ref[row] * k_ref[row, 32:33, :]).astype(BF16)
             kind = 1 if row % 8 == 0 else 0
-            o = lax.dot_general(ib_ref[kind], both, NT, preferred_element_type=F32)
-            z_ref[:, row * 16 : row * 16 + 16, :] = o.astype(BF16).reshape(N, 16, 256)
-        for i in range(N):
-            o = lax.dot_general(ia_ref[...], z_ref[i], NN, preferred_element_type=F32)
-            g_ref[i] += o[:, :128] * o[:, 128:]
+            o = lax.dot_general(ib_ref[kind], one, NT, preferred_element_type=F32)
+            z_ref[:, row * 16 : row * 16 + 16, :CELLS] = o.astype(BF16).reshape(N, 16, CELLS)
+        fluid = fluid_ref[c] == 0
+
+        def finish(peer):
+            for h in range(2):
+                i = 2 * peer + h
+                loss = lax.dot_general(
+                    ia_ref[...], z_ref[i, :, :CELLS], NN, preferred_element_type=F32
+                )
+                gain = g_ref[i].T
+                gain = gain[:CELLS] + gain[CELLS:]
+                x = x_ref[c, peer, :, h * 256 : h * 256 + 256]
+                change = gain - x * loss.T
+                r_ref[c, peer, :, h * 256 : h * 256 + 256] = jnp.where(
+                    fluid, x + collision_timestep * change, x
+                )
+
+        def one(s, _):
+            peer = lax.rem(me + s, GROUP)
+            finish(peer)
+            back(c, s).start()
+            return 0
+
+        lax.fori_loop(1, GROUP, one, 0)
+        finish(me)
+        pltpu.make_async_copy(r_ref.at[c, me], out_ref.at[me, c], own_sem.at[c]).start()
         return 0
 
-    lax.fori_loop(0, DIRS, direction, 0)
-    for row in range(N):
-        one = (s_ref[row] * k_ref[row, 32:33, :]).astype(BF16)
-        kind = 1 if row % 8 == 0 else 0
-        o = lax.dot_general(ib_ref[kind], one, NT, preferred_element_type=F32)
-        z_ref[:, row * 16 : row * 16 + 16, :128] = o.astype(BF16).reshape(N, 16, 128)
-    fluid = fluid_ref[...] == 0
-    for i in range(N):
-        loss = lax.dot_general(ia_ref[...], z_ref[i, :, :128], NN, preferred_element_type=F32)
-        lanes = slice((i % 2) * 256, (i % 2) * 256 + 256)
-        x = x_ref[i // 2, :, lanes]
-        change = g_ref[i].T - x * loss.T
-        out_ref[i // 2, :, lanes] = jnp.where(fluid, x + collision_timestep * change, x)
+    def back(c, s):
+        peer = lax.rem(me + s, GROUP)
+        return remote(
+            r_ref.at[c, peer], out_ref.at[me, c], back_send.at[c, s], back_recv.at[c, s], peer
+        )
+
+    lax.fori_loop(0, CHUNKS, chunk, 0)
+    for c in range(CHUNKS):
+        pltpu.make_async_copy(r_ref.at[c, me], out_ref.at[me, c], own_sem.at[c]).wait()
+        for s in range(1, GROUP):
+            if c:
+                send(c, s).wait_send()
+            back(c, s).wait()
 
 
 def constant_tables():
     fr, fi, ir, ii = line_tables()
     to = lambda t: np.asarray(t, np.float32).astype(BF16)
-    return (fr, fi), tuple(
-        to(t) for t in (j_table(fr, fi), k_tables(fr, fi), inverse_i_tables(ir, ii), inverse_jk_table(ir, ii))
-    ), packing_index()
-
-
-def collide(x, cells, packed, lines, tables):
+    tables = (j_table(fr, fi), k_tables(fr, fi), inverse_i_tables(ir, ii), inverse_jk_table(ir, ii))
+    return (fr, fi), tuple(to(t) for t in tables), packing_index()
+
+
+def step(moved, types, index, first, second, loss, lines, tables):
+    hbm = pl.BlockSpec(memory_space=pl.ANY)
+    vmem = pl.BlockSpec(memory_space=pltpu.VMEM)
+    dma = pltpu.SemaphoreType.DMA
     return pl.pallas_call(
-        functools.partial(collide_body, *lines),
-        out_shape=jax.ShapeDtypeStruct((8, 128, 512), F32),
+        functools.partial(step_body, *lines),
+        out_shape=jax.ShapeDtypeStruct(moved.shape, F32),
+        in_specs=[hbm, vmem, vmem] + [hbm] * 7,
+        out_specs=hbm,
         scratch_shapes=[
-            pltpu.VMEM((9, 128, 512), BF16),
-            pltpu.VMEM((9, 512, 128), BF16),
-            pltpu.VMEM((N, 256, 128), BF16),
-            pltpu.VMEM((N, 128, 256), F32),
+            pltpu.VMEM((CHUNKS, GROUP, CELLS, 512), F32),
+            pltpu.VMEM((CHUNKS, GROUP, CELLS, 512), F32),
+            pltpu.VMEM((48, 4096), F32),
+            pltpu.VMEM((N, 48, 256), F32),
+            pltpu.VMEM((4, 512, 256), BF16),
+            pltpu.VMEM((N, 48, 256), F32),
+            pltpu.VMEM((512, 512), BF16),
+            pltpu.VMEM((4, 256, 512), BF16),
+            pltpu.VMEM((2, 256, 256), BF16),
+            pltpu.VMEM((256, 256), BF16),
+            pltpu.VMEM((9 * CELLS, 512), BF16),
+            pltpu.VMEM((512, 9 * CELLS), BF16),
+            pltpu.VMEM((N, 256, CELLS), BF16),
+            pltpu.VMEM((N, CELLS, 256), F32),
             pltpu.VMEM((N, 256, 256), BF16),
             pltpu.VMEM((N, 256, 128), F32),
+            dma((CHUNKS, GROUP)),
+            dma((CHUNKS, GROUP)),
+            dma((CHUNKS, GROUP)),
+            dma((CHUNKS, GROUP)),
+            dma((CHUNKS,)),
+            dma((7,)),
         ],
-        compiler_params=pltpu.CompilerParams(vmem_limit_bytes=40 << 20),
-        cost_estimate=pl.CostEstimate(flops=18 << 30, bytes_accessed=8 << 20, transcendentals=0),
-        name="collide",
-    )(x, cells, packed, *tables)
+        compiler_params=pltpu.CompilerParams(
+            vmem_limit_bytes=40 << 20, collective_id=0, has_side_effects=True
+        ),
+        name="step",
+    )(moved, types, index, first, second, loss, *tables)
 
 
 def components(nvel):
@@ -318,12 +446,18 @@
     rimmed = jnp.concatenate([below, walled, above], axis=1)
     padded = jnp.pad(rimmed, ((1, 1), (0, 0), (0, 0)))
     moved = jnp.where(fluid, walled + transport(padded, here(along_x), here(along_y)), walled)
-    sent = lax.all_to_all(moved.reshape(groups, slab, cols, block), "vel", 0, 0, tiled=True)
-    packed = pack_kernels(first, second, loss, one_hot)
-    types = lax.dynamic_slice_in_dim(cell_type, rank * slab, slab, 0).reshape(slab * cols, 1)
-    done = collide(sent.reshape(groups, slab * cols, block), types, packed, lines, tables)
-    back = lax.all_to_all(done.reshape(groups, slab, cols, block), "vel", 0, 0, tiled=True)
-    return back.reshape(rows, cols, block)
+    types = lax.dynamic_slice_in_dim(cell_type, rank * slab, slab, 0)
+    done = step(
+        moved.reshape(groups, CHUNKS, CELLS, block),
+        types.reshape(CHUNKS, CELLS, 1),
+        one_hot,
+        first,
+        second,
+        jnp.broadcast_to(loss[None], (8, 4096)),
+        lines,
+        tables,
+    )
+    return done.reshape(rows, cols, block)
 
 
 def solution(mesh):

time: 129 us -> 99.1 us (0.77)
  blocking collectives: 33.4 us -> 0 us
  Pallas kernels: 31.5 us -> 62.8 us
  waiting for transfers between devices: 31.1 us -> 9.42 us
  local copies, waits for them, and re-layouts: 8.32 us -> 4.26 us
  starting transfers between devices: 17.3 us -> 13.5 us
  other arithmetic: 7.23 us -> 8.66 us
    all_to_all x1 -> x0, blocking collectives: 33.4 us -> none  [on_device(): lax.all_to_all(done.reshape(groups, slab, cols, block), 'vel', 0, 0, tile...]
    pallas_call x2 -> x1, Pallas kernels: 31.5 us -> 62.8 us  [step(): pl.pallas_call(functools.partial(step_body, *lines), out_shape=jax.ShapeD...]
    all_to_all x1 -> x0, waiting for transfers between devices: 21.4 us -> none  [on_device(): lax.all_to_all(moved.reshape(groups, slab, cols, block), 'vel', 0, 0, til...]
    all_to_all x1 -> x0, starting transfers between devices: 3.79 us -> none  [on_device(): lax.all_to_all(moved.reshape(groups, slab, cols, block), 'vel', 0, 0, til...]
    unnamed x19 -> x23, local copies, waits for them, and re-layouts: 4.51 us -> 1.73 us
    reshape x2 -> x1, local copies, waits for them, and re-layouts: 2.59 us -> 0.08 us  [on_device(): types.reshape(CHUNKS, CELLS, 1)]
    select_n x1, other arithmetic: 1.32 us -> 2.98 us  [on_device(): walled = jnp.where(fluid, distribution, density[:, :, None] * wall)]
  transfers between devices with their start and end apart: 4 -> 3, of which waited for: 4 -> 3; matrix products, arithmetic and copies ran while one was open for 2% -> 3% of each run, Pallas kernels for 3% -> 0%
where the time goes in v2:
time: 99.1 us; the launch traced here: 98.8 us
  Pallas kernels  62.8 us (63%)
  starting transfers between devices  13.5 us (14%)
  waiting for transfers between devices  9.42 us (10%)
  other arithmetic  8.66 us (9%)
  local copies, waits for them, and re-layouts  4.26 us (4%)
    pallas_call x1, Pallas kernels, step(): pl.pallas_call(functools.partial(step_body, *lines), out_shape=jax.ShapeD...  62.8 us
    ppermute x1, starting transfers between devices, on_device(): below = lax.ppermute(walled[:, cols - 1:], 'cell', up)  6.52 us
    ppermute x1, waiting for transfers between devices, on_device(): above = lax.ppermute(walled[:, :1], 'cell', [(b, a) for a, b in up])  5.9 us
    all_to_all x1, starting transfers between devices, on_device(): lax.all_to_all(jnp.broadcast_to(partial[None], (groups, rows, cols)), 've...  5.03 us
    select_n x1, other arithmetic, on_device(): walled = jnp.where(fluid, distribution, density[:, :, None] * wall)  2.98 us
    all_to_all x1, waiting for transfers between devices, on_device(): lax.all_to_all(jnp.broadcast_to(partial[None], (groups, rows, cols)), 've...  2.4 us
  transfers between devices with their start and end apart: 3, of which 3 were waited for; matrix products, arithmetic and copies ran while one was open for 3% of the time, Pallas kernels for 0%

profile of v2, /device:TPU:33, one launch (start us, length us, event | category | flops | bytes accessed | tf_op | source)
XLA Modules:
  0.0 98.8 jit_solution(17882856445734250786)
XLA Ops:
  0.0 0.0 copy-start.8
  0.0 1.8 %reduce_sum.36 = f32[128,8]{1,0:T(8,128)S(1)} reduce(f32[128,8,512]{2,1,0:T(8,128)} %param.10, f32[]{:T(128)} %constant.11.clone.1), dimensions={2}, to_apply=%region_0.0 | reduce | flops 523264 | bytes 2101252 | tf_op jit(solution)/shard_map/reduce_sum | solution.py:434
  1.9 0.6 broadcast_in_dim.79
  2.5 5.0 %all-to-all-start = ((f32[8,128,8]{1,2,0:T(8,128)}), f32[8,128,8]{1,2,0:T(8,128)S(1)}, u32[]{:S(2)}, u32[]{:S(2)}) async-start(f32[8,128,8]{1,2,0:T(8,128)} %broadcast_in_dim.79), calls=%async_computation | async-start | bytes 65536 | tf_op jit(solution)/shard_map/all_to_all | solution.py:435
  7.6 0.1 broadcast_in_dim.82
  7.7 0.1 tile.55
  7.8 0.1 broadcast_bitcast_fusion.1
  7.8 0.1 tile.62
  8.0 0.1 tile.59
  8.1 0.0 copy-done.8
  8.1 0.8 exponential_reduce_fusion
  8.9 1.4 %dynamic-slice_maximum_fusion = (f32[512]{0:T(512)S(1)}, f32[512]{0:T(512)S(1)}, f32[512]{0:T(512)S(1)}, f32[512]{0:T(512)S(1)}, f32[512]{0:T(512)S(1)}, /*index=5*/f32[512]{0:T(512)S(1)}) fusion(f32[4096]{0:T(1024)S(1)} %bitcast.13, s32[]{:T(128)S(6)} %select_n.20, f32[]{:T(128)} %get-tuple-element.21, f32[4096]{0:T(1024)S(1)} %tile.59, ...), kind=kLoop, calls=%fused_computation.41 | loop fusion | flops 9728 | bytes 22540 | tf_op jit(solution)/shard_map/max | solution.py:419
  10.3 2.4 %all-to-all-done = f32[8,128,8]{1,2,0:T(8,128)S(1)} async-done(((f32[8,128,8]{1,2,0:T(8,128)}), f32[8,128,8]{1,2,0:T(8,128)S(1)}, u32[]{:S(2)}, u32[]{:S(2)}) %all-to-all-start) | async-done | bytes 32800 | tf_op jit(solution)/shard_map/all_to_all | solution.py:435
  12.7 3.0 %copy_select_fusion = f32[128,8,512]{2,0,1:T(8,128)S(1)} fusion(f32[128,8,512]{2,1,0:T(8,128)} %param.10, f32[512]{0:T(512)S(1)} %get-tuple-element.11, f32[512]{0:T(512)S(1)} %get-tuple-element.12, f32[128,8]{0,1:T(8,128)S(1)} %reduce_sum.37, pred[128,8]{0,1:T(8,128)(4,1)S(1)} %get-tuple-element.16, pred[128,8]{0,1:T(8,128)(4,1)S(1)} %get-tuple-element.15), kind=kLoop, calls=%fused_computation.20 | loop fusion | flops 1572864 | bytes 4204544 | tf_op jit(solution)/shard_map/jit(_where)/select_n | solution.py:441
  15.7 6.5 %collective-permute-start = (f32[128,1,512]{2,0,1:T(8,128)S(1)}, f32[128,1,512]{2,0,1:T(8,128)S(1)}, u32[]{:S(2)}, u32[]{:S(2)}) collective-permute-start(f32[128,1,512]{2,0,1:T(8,128)S(1)} %get-tuple-element.5), channel_id=1, source_target_pairs={{0,8},{8,16},{16,24},{24,32},{32,40},{40,48},{48,56},{56,64},{64,7... | collective-permute-start | bytes 786440 | tf_op jit(solution)/shard_map/ppermute | solution.py:444
  22.2 1.9 %collective-permute-start.1 = (f32[128,1,512]{2,0,1:T(8,128)S(1)}, f32[128,1,512]{2,0,1:T(8,128)S(1)}, u32[]{:S(2)}, u32[]{:S(2)}) collective-permute-start(f32[128,1,512]{2,0,1:T(8,128)S(1)} %get-tuple-element.6), channel_id=1, source_target_pairs={{8,0},{16,8},{24,16},{32,24},{40,32},{48,40},{56,48},{64,56},{72,6... | collective-permute-start | bytes 786440 | tf_op jit(solution)/shard_map/ppermute | solution.py:445
  24.2 0.1 constant_dynamic-slice_fusion
  24.2 0.1 copy.31
  24.3 0.1 reshape.43.fluid_ref
  24.4 1.1 %collective-permute-done = f32[128,1,512]{2,0,1:T(8,128)S(1)} collective-permute-done((f32[128,1,512]{2,0,1:T(8,128)S(1)}, f32[128,1,512]{2,0,1:T(8,128)S(1)}, u32[]{:S(2)}, u32[]{:S(2)}) %collective-permute-start) | collective-permute-done | bytes 262176 | tf_op jit(solution)/shard_map/ppermute | solution.py:444
  25.5 5.9 %collective-permute-done.1 = f32[128,1,512]{2,0,1:T(8,128)S(1)} collective-permute-done((f32[128,1,512]{2,0,1:T(8,128)S(1)}, f32[128,1,512]{2,0,1:T(8,128)S(1)}, u32[]{:S(2)}, u32[]{:S(2)}) %collective-permute-start.1) | collective-permute-done | bytes 262176 | tf_op jit(solution)/shard_map/ppermute | solution.py:445
  31.4 0.4 select_maximum_fusion
  31.8 1.3 %add_select_fusion = f32[128,8,512]{2,0,1:T(8,128)S(1)} fusion(f32[128,8,512]{2,0,1:T(8,128)S(1)} %copy_select_fusion, f32[128,1,512]{2,0,1:T(8,128)S(1)} %collective-permute-done.1, f32[128,1,512]{2,0,1:T(8,128)S(1)} %collective-permute-done, f32[130,10,512]{2,0,1:T(8,128)S(1)} %select_maximum_fusion, f32[512]{0:T(512)S(1)} %get-tuple-element.14, ...), kind=kLoop, calls=%fused_computation.2 | loop fusion | flops 8388608 | bytes 8922112 | tf_op jit(solution)/shard_map/jit(_where)/select_n | solution.py:448
  33.1 0.0 copy-start.7
  33.1 0.0 copy-start
  33.1 0.0 copy-start.1
  33.1 0.0 copy-start.2
  33.1 0.0 copy-start.3
  33.2 0.0 copy-start.4
  33.2 0.0 copy-start.5
  33.2 0.0 copy-start.6
  33.2 1.2 %copy.30 = f32[128,8,512]{2,1,0:T(8,128)S(1)} copy(f32[128,8,512]{2,0,1:T(8,128)S(1)} %add_select_fusion) | data formatting | bytes 4194304 | tf_op jit(solution)/shard_map/jit(_where)/select_n | solution.py:448
  34.4 0.0 copy-done.7
  34.4 0.0 copy-done
  34.5 0.0 copy-done.1
  34.5 0.1 copy-done.2
  34.5 0.1 copy-done.3
  34.6 0.1 copy-done.4
  34.7 0.0 copy-done.5
  34.7 0.0 copy-done.6
  34.7 62.8 %step.1 = f32[8,2,64,512]{3,2,1,0:T(8,128)S(1)} custom-call(f32[8,2,64,512]{3,2,1,0:T(8,128)S(1)} %bitcast.8, s32[2,64,1]{2,1,0:T(8,128)S(1)} %reshape.43.fluid_ref, s32[4,2,256]{2,1,0:T(2,128)S(1)} %copy-done.6, f32[16,4096]{1,0:T(8,128)S(1)} %copy-done.2, f32[16,4096]{1,0:T(8,128)S(1)} %copy-done.3, f32[8,4096]{1,0:T(8,128)S(1)} %broadcast_in_dim.87.loss_ref, ...), custom_call_target="tpu_custom_call" | custom-call | tf_op jit(solution)/shard_map/step/pallas_call | solution.py:359
  97.5 1.3 %copy.37 = f32[128,8,512]{2,1,0:T(8,128)} copy(f32[128,8,512]{2,1,0:T(8,128)S(1)} %bitcast.9) | data formatting | bytes 4194304
  (16 shorter events, 0.2 us)
Async XLA Ops:
  0.0 8.1 %copy-start.8 = (s32[128,8]{0,1:T(8,128)S(1)}, s32[128,8]{0,1:T(8,128)}, u32[]{:S(2)}) copy-start(s32[128,8]{0,1:T(8,128)} %param.11) | copy-start | bytes 12292
  2.5 10.1 %all-to-all-start = ((f32[8,128,8]{1,2,0:T(8,128)}), f32[8,128,8]{1,2,0:T(8,128)S(1)}, u32[]{:S(2)}, u32[]{:S(2)}) async-start(f32[8,128,8]{1,2,0:T(8,128)} %broadcast_in_dim.79), calls=%async_computation | async-start | bytes 65536 | tf_op jit(solution)/shard_map/all_to_all | solution.py:435
  15.7 9.8 %collective-permute-start = (f32[128,1,512]{2,0,1:T(8,128)S(1)}, f32[128,1,512]{2,0,1:T(8,128)S(1)}, u32[]{:S(2)}, u32[]{:S(2)}) collective-permute-start(f32[128,1,512]{2,0,1:T(8,128)S(1)} %get-tuple-element.5), channel_id=1, source_target_pairs={{0,8},{8,16},{16,24},{24,32},{32,40},{40,48},{48,56},{56,64},{64,7... | collective-permute-start | bytes 786440 | tf_op jit(solution)/shard_map/ppermute | solution.py:444
  22.2 9.2 %collective-permute-start.1 = (f32[128,1,512]{2,0,1:T(8,128)S(1)}, f32[128,1,512]{2,0,1:T(8,128)S(1)}, u32[]{:S(2)}, u32[]{:S(2)}) collective-permute-start(f32[128,1,512]{2,0,1:T(8,128)S(1)} %get-tuple-element.6), channel_id=1, source_target_pairs={{8,0},{16,8},{24,16},{32,24},{40,32},{48,40},{56,48},{64,56},{72,6... | collective-permute-start | bytes 786440 | tf_op jit(solution)/shard_map/ppermute | solution.py:445
  33.1 1.3 %copy-start.7 = (f32[4096]{0:T(1024)S(1)}, f32[4096]{0:T(1024)}, u32[]{:S(2)}) copy-start(f32[4096]{0:T(1024)} %param.14) | copy-start | bytes 49156
  33.1 1.3 %copy-start = (bf16[4,256,512]{2,1,0:T(8,128)(2,1)S(1)}, bf16[4,256,512]{2,1,0:T(8,128)(2,1)}, u32[]{:S(2)}) copy-start(bf16[4,256,512]{2,1,0:T(8,128)(2,1)} %constant.55.clone.kt_hbm) | copy-start | bytes 3145732
  33.1 1.4 %copy-start.1 = (bf16[512,512]{1,0:T(8,128)(2,1)S(1)}, bf16[512,512]{1,0:T(8,128)(2,1)}, u32[]{:S(2)}) copy-start(bf16[512,512]{1,0:T(8,128)(2,1)} %constant.54.clone.jt_hbm) | copy-start | bytes 1572868
  33.1 1.4 %copy-start.2 = (f32[16,4096]{1,0:T(8,128)S(1)}, f32[16,4096]{1,0:T(8,128)}, u32[]{:S(2)}) copy-start(f32[16,4096]{1,0:T(8,128)} %first_ref.1) | copy-start | bytes 786436
  33.1 1.5 %copy-start.3 = (f32[16,4096]{1,0:T(8,128)S(1)}, f32[16,4096]{1,0:T(8,128)}, u32[]{:S(2)}) copy-start(f32[16,4096]{1,0:T(8,128)} %second_ref.1) | copy-start | bytes 786436
  33.2 1.5 %copy-start.4 = (bf16[2,256,256]{2,1,0:T(8,128)(2,1)S(1)}, bf16[2,256,256]{2,1,0:T(8,128)(2,1)}, u32[]{:S(2)}) copy-start(bf16[2,256,256]{2,1,0:T(8,128)(2,1)} %constant.56.clone.ib_hbm) | copy-start | bytes 786436
  33.2 1.6 %copy-start.5 = (bf16[256,256]{1,0:T(8,128)(2,1)S(1)}, bf16[256,256]{1,0:T(8,128)(2,1)}, u32[]{:S(2)}) copy-start(bf16[256,256]{1,0:T(8,128)(2,1)} %constant.57.clone.ia_hbm) | copy-start | bytes 393220
  33.2 1.6 %copy-start.6 = (s32[4,2,256]{2,1,0:T(2,128)S(1)}, s32[4,2,256]{2,1,0:T(2,128)}, u32[]{:S(2)}) copy-start(s32[4,2,256]{2,1,0:T(2,128)} %constant.53.clone.index_ref) | copy-start | bytes 24580

commit v3 on v2

--- a/solution.py
+++ b/solution.py
@@ -214,24 +214,56 @@
     )
 
 
+def cell_rows():
+    level = (2.0 * np.arange(N) - (N - 1)) / (N - 1)
+    x, y, z = np.meshgrid(level, level, level, indexing="ij")
+    still = np.exp(-4.5 * (x * x + y * y + z * z))
+    moving = np.exp(-0.5 * ((3.0 * x - 1.0) ** 2 + 9.0 * y * y + 9.0 * z * z))
+    zero = np.zeros_like(x)
+    rows = [
+        np.maximum(x, 0), np.minimum(x, 0), np.maximum(y, 0), np.minimum(y, 0),
+        still / still.sum(), moving / moving.sum(), zero, zero,
+    ]
+    out = np.stack([r.reshape(GROUP, 512) for r in rows], axis=1)
+    return np.asarray(out, np.float32)
+
+
 def step_body(
-    fr, fi, moved_ref, fluid_ref, index_ref, first_ref, second_ref, loss_ref,
+    fr, fi, dist_ref, type_ref, index_ref, rows_hbm, first_ref, second_ref, loss_ref,
     jt_hbm, kt_hbm, ib_hbm, ia_hbm, out_ref,
+    d_ref, w_ref, t_ref, e_ref, h_ref, msg_ref, in_ref, row_ref, moved_ref,
     x_ref, r_ref, all_ref, mid_ref, hot_ref, k_ref, jt_ref, kt_ref, ib_ref, ia_ref,
     x1_ref, x2_ref, sr_ref, s_ref, z_ref, g_ref,
     send_sem, recv_sem, back_send, back_recv, own_sem, load_sem,
+    dist_sem, msg_send, msg_recv, edge_send, edge_recv,
 ):
     me = lax.axis_index("vel")
+    cell = lax.axis_index("cell")
+    cells = lax.axis_size("cell")
+    sides = (lax.rem(cell + cells - 1, cells), lax.rem(cell + 1, cells))
     barrier = pltpu.get_barrier_semaphore()
-    for s in range(1, GROUP):
+
+    def greet(place, peer):
         pl.semaphore_signal(
-            barrier, inc=1, device_id={"vel": lax.rem(me + s, GROUP)},
+            barrier, inc=1, device_id={"cell": place, "vel": peer},
             device_id_type=pl.DeviceIdType.MESH,
         )
+
+    for s in range(GROUP):
+        peer = lax.rem(me + s, GROUP)
+        if s:
+            greet(cell, peer)
+        for place in sides:
+            greet(place, peer)
+    slabs = [
+        pltpu.make_async_copy(
+            dist_ref.at[pl.ds(t * 128, 128)], d_ref.at[pl.ds(t * 128, 128)], dist_sem.at[t]
+        )
+        for t in range(GROUP)
+    ]
     loads = [
         pltpu.make_async_copy(first_ref, all_ref.at[0:16], load_sem.at[0]),
         pltpu.make_async_copy(second_ref, all_ref.at[16:32], load_sem.at[1]),
-        pltpu.make_async_copy(loss_ref, all_ref.at[32:40], load_sem.at[2]),
     ]
     tables = [
         pltpu.make_async_copy(jt_hbm, jt_ref, load_sem.at[3]),
@@ -239,34 +271,133 @@
         pltpu.make_async_copy(ib_hbm, ib_ref, load_sem.at[5]),
         pltpu.make_async_copy(ia_hbm, ia_ref, load_sem.at[6]),
     ]
-    own = [
-        pltpu.make_async_copy(moved_ref.at[me, c], x_ref.at[c, me], own_sem.at[c])
-        for c in range(CHUNKS)
+    profile = pltpu.make_async_copy(rows_hbm.at[me], row_ref, load_sem.at[7])
+    for copy in slabs + [profile] + loads + tables:
+        copy.start()
+
+    lane = lax.broadcasted_iota(jnp.int32, (8, 128), 1)
+    total = jnp.zeros((8, 128), F32)
+    for t in range(GROUP):
+        slabs[t].wait()
+        for u in range(16):
+            x = t * 16 + u
+            v = d_ref[x * 8 : x * 8 + 8, :]
+            v = (v[:, :128] + v[:, 128:256]) + (v[:, 256:384] + v[:, 384:])
+            total = jnp.where(lane == x, jnp.sum(v, axis=1, keepdims=True), total)
+            for side in range(2):
+                at = x * 8 + 7 * side
+                e_ref[side, x : x + 1, :] = d_ref[at : at + 1, :]
+    kinds = type_ref[...].astype(F32)
+    msg_ref[0:8, :] = total
+    msg_ref[8:16, :] = kinds
+    in_ref[0, me] = msg_ref[...]
+    pl.semaphore_wait(barrier, 3 * GROUP - 1)
+
+    def reach(src, dst, send, recv, place, peer):
+        return pltpu.make_async_remote_copy(
+            src_ref=src, dst_ref=dst, send_sem=send, recv_sem=recv,
+            device_id={"cell": place, "vel": peer}, device_id_type=pl.DeviceIdType.MESH,
+        )
+
+    edges = [
+        reach(e_ref.at[side], h_ref.at[1 - side], edge_send.at[side], edge_recv.at[side], sides[side], me)
+        for side in range(2)
     ]
-    for copy in loads + tables + own:
+    notes = []
+    for s in range(GROUP):
+        peer = lax.rem(me + s, GROUP)
+        for kind, place in ((0, cell), (2, sides[0]), (1, sides[1])):
+            if kind or s:
+                notes.append(
+                    reach(
+                        msg_ref, in_ref.at[kind, me], msg_send.at[kind, s], msg_recv.at[kind, s],
+                        place, peer,
+                    )
+                )
+    for copy in edges + notes:
         copy.start()
-    pl.semaphore_wait(barrier, GROUP - 1)
+
+    for copy in loads:
+        copy.wait()
+    all_ref[32:48] = jnp.broadcast_to(loss_ref[...], (16, 4096))
+    pack(index_ref, all_ref, mid_ref, hot_ref, k_ref)
+    profile.wait()
+    for copy in notes + edges:
+        copy.wait()
+    still, moving = row_ref[4:5, :], row_ref[5:6, :]
+
+    def gathered(kind):
+        v = in_ref[kind]
+        v = (v[0:2] + v[2:4]) + (v[4:6] + v[6:8])
+        return (v[0] + v[1])[0:8]
+
+    for side in range(2):
+        density = gathered(1 + side).T[:, 7 - 7 * side : 8 - 7 * side]
+        kind = in_ref[1 + side, 0, 8:16, :].T[:, 7 - 7 * side : 8 - 7 * side]
+        wall = density * jnp.where(kind == 1.0, still, moving)
+        inside = cell > 0 if side == 0 else cell < cells - 1
+        h_ref[side] = jnp.where(kind == 0.0, h_ref[side], wall) * jnp.where(inside, 1.0, 0.0)
+    density = gathered(0)
+    w_ref[0:8, :] = jnp.zeros((8, 512), F32)
+    w_ref[1032:1040, :] = jnp.zeros((8, 512), F32)
+
+    def walled(t, _):
+        for u in range(8):
+            x = t * 8 + u
+            at = pl.ds(pl.multiple_of(x * 8, 8), 8)
+            here = lane == x
+            kind = jnp.sum(jnp.where(here, kinds, 0.0), axis=1, keepdims=True)
+            dense = jnp.sum(jnp.where(here, density, 0.0), axis=1, keepdims=True)
+            wall = dense * jnp.where(kind == 1.0, still, moving)
+            w = jnp.where(kind == 0.0, d_ref[at, :], wall)
+            w_ref[pl.ds(pl.multiple_of(x * 8 + 8, 8), 8), :] = w
+            t_ref[at, :] = jnp.broadcast_to(kind, (8, 128))
+        return 0
+
+    lax.fori_loop(0, 16, walled, 0)
+    depth = lax.broadcasted_iota(jnp.int32, (8, 512), 0)
+
+    def transport(peer, c, out_ref, *place):
+        for u in range(8):
+            x = peer * 16 + c * 8 + u
+            low = w_ref[pl.ds(pl.multiple_of(x * 8, 8), 8), :]
+            w = w_ref[pl.ds(pl.multiple_of(x * 8 + 8, 8), 8), :]
+            high = w_ref[pl.ds(pl.multiple_of(x * 8 + 16, 8), 8), :]
+            left = jnp.where(depth == 0, h_ref[0, pl.ds(x, 1), :], pltpu.roll(w, 1, 0))
+            right = jnp.where(depth == 7, h_ref[1, pl.ds(x, 1), :], pltpu.roll(w, 7, 0))
+            flow = row_ref[0:1, :] * (w - low) + row_ref[1:2, :] * (high - w)
+            flow = flow + row_ref[2:3, :] * (w - left) + row_ref[3:4, :] * (right - w)
+            kind = t_ref[pl.ds(pl.multiple_of(x * 8, 8), 8), :]
+            kind = jnp.concatenate([kind] * 4, axis=1)
+            out_ref[*place, u * 8 : u * 8 + 8, :] = jnp.where(kind == 0.0, w - courant * flow, w)
 
     def send(c, s):
         peer = lax.rem(me + s, GROUP)
         return remote(
-            moved_ref.at[peer, c], x_ref.at[c, me], send_sem.at[c, s], recv_sem.at[c, s], peer
-        )
-
-    def start(c):
-        for s in range(1, GROUP):
-            send(c, s).start()
-
-    start(0)
-    for copy in loads:
-        copy.wait()
-    all_ref[40:48] = jnp.zeros((8, 4096), F32)
-    pack(index_ref, all_ref, mid_ref, hot_ref, k_ref)
-    for copy in tables + own:
+            moved_ref.at[c, peer], x_ref.at[c, me], send_sem.at[c, s], recv_sem.at[c, s], peer
+        )
+
+    def first_half(s, _):
+        peer = lax.rem(me + s, GROUP)
+        transport(peer, 0, moved_ref, 0, peer)
+        send(0, s).start()
+        return 0
+
+    def second_half(s, _):
+        peer = lax.rem(me + s, GROUP)
+        transport(peer, 1, moved_ref, 1, peer)
+        return 0
+
+    lax.fori_loop(1, GROUP, first_half, 0)
+    lax.fori_loop(1, GROUP, second_half, 0)
+    for c in range(CHUNKS):
+        transport(me, c, x_ref, c, me)
+    for copy in tables:
         copy.wait()
     for s in range(1, GROUP):
         send(0, s).wait_send()
-    start(1)
+    for s in range(1, GROUP):
+        send(1, s).start()
 
     def chunk(c, _):
         for s in range(1, GROUP):
@@ -303,7 +434,8 @@
             kind = 1 if row % 8 == 0 else 0
             o = lax.dot_general(ib_ref[kind], one, NT, preferred_element_type=F32)
             z_ref[:, row * 16 : row * 16 + 16, :CELLS] = o.astype(BF16).reshape(N, 16, CELLS)
-        fluid = fluid_ref[c] == 0
+        at = pl.ds(pl.multiple_of(me * 128 + c * CELLS, CELLS), CELLS)
+        fluid = jnp.concatenate([t_ref[at, :]] * 2, axis=1) == 0.0
 
         def finish(peer):
             for h in range(2):
@@ -352,16 +484,25 @@
     return (fr, fi), tuple(to(t) for t in tables), packing_index()
 
 
-def step(moved, types, index, first, second, loss, lines, tables):
+def step(distribution, cell_type, index, profiles, first, second, loss, lines, tables):
     hbm = pl.BlockSpec(memory_space=pl.ANY)
     vmem = pl.BlockSpec(memory_space=pltpu.VMEM)
     dma = pltpu.SemaphoreType.DMA
     return pl.pallas_call(
         functools.partial(step_body, *lines),
-        out_shape=jax.ShapeDtypeStruct(moved.shape, F32),
-        in_specs=[hbm, vmem, vmem] + [hbm] * 7,
+        out_shape=jax.ShapeDtypeStruct((GROUP, CHUNKS, CELLS, 512), F32),
+        in_specs=[hbm, vmem, vmem] + [hbm] * 3 + [vmem] + [hbm] * 4,
         out_specs=hbm,
         scratch_shapes=[
+            pltpu.VMEM((1024, 512), F32),
+            pltpu.VMEM((1040, 512), F32),
+            pltpu.VMEM((1024, 128), F32),
+            pltpu.VMEM((2, 128, 512), F32),
+            pltpu.VMEM((2, 128, 512), F32),
+            pltpu.VMEM((16, 128), F32),
+            pltpu.VMEM((3, GROUP, 16, 128), F32),
+            pltpu.VMEM((8, 512), F32),
+            pltpu.VMEM((CHUNKS, GROUP, CELLS, 512), F32),
             pltpu.VMEM((CHUNKS, GROUP, CELLS, 512), F32),
             pltpu.VMEM((CHUNKS, GROUP, CELLS, 512), F32),
             pltpu.VMEM((48, 4096), F32),
@@ -383,88 +524,40 @@
             dma((CHUNKS, GROUP)),
             dma((CHUNKS, GROUP)),
             dma((CHUNKS,)),
-            dma((7,)),
+            dma((8,)),
+            dma((GROUP,)),
+            dma((3, GROUP)),
+            dma((3, GROUP)),
+            dma((2,)),
+            dma((2,)),
         ],
         compiler_params=pltpu.CompilerParams(
-            vmem_limit_bytes=40 << 20, collective_id=0, has_side_effects=True
+            vmem_limit_bytes=62 << 20, collective_id=0, has_side_effects=True
         ),
         name="step",
-    )(moved, types, index, first, second, loss, *tables)
-
-
-def components(nvel):
-    levels = (2.0 * jnp.arange(nvel, dtype=F32) - (nvel - 1)) / (nvel - 1)
-    along_x = jnp.repeat(levels, nvel * nvel)
-    along_y = jnp.tile(jnp.repeat(levels, nvel), nvel)
-    along_z = jnp.tile(levels, nvel * nvel)
-    return along_x, along_y, along_z
-
-
-def wall_tables(along_x, along_y, along_z):
-    still_wall = jnp.exp(-4.5 * (along_x * along_x + along_y * along_y + along_z * along_z))
-    still_wall = still_wall / jnp.sum(still_wall)
-    moving = jnp.exp(
-        -0.5 * ((3.0 * along_x - 1.0) ** 2 + 9.0 * along_y * along_y + 9.0 * along_z * along_z)
-    )
-    moving = moving / jnp.sum(moving)
-    return still_wall, moving
-
-
-def transport(padded, along_x, along_y):
-    center = padded[1:-1, 1:-1]
-    back_x = center - padded[:-2, 1:-1]
-    front_x = padded[2:, 1:-1] - center
-    back_y = center - padded[1:-1, :-2]
-    front_y = padded[1:-1, 2:] - center
-    plus_x = jnp.maximum(along_x, 0.0)[None, None, :]
-    minus_x = jnp.minimum(along_x, 0.0)[None, None, :]
-    plus_y = jnp.maximum(along_y, 0.0)[None, None, :]
-    minus_y = jnp.minimum(along_y, 0.0)[None, None, :]
-    return -courant * (plus_x * back_x + minus_x * front_x + plus_y * back_y + minus_y * front_y)
-
-
-def on_device(lines, tables, one_hot, distribution, cell_type, first, second, loss):
-    rows, cols, block = distribution.shape
-    groups = lax.axis_size("vel")
-    rank = lax.axis_index("vel")
-    slab = rows // groups
-    along_x, along_y, along_z = components(N)
-    still, moving = wall_tables(along_x, along_y, along_z)
-    here = lambda t: lax.dynamic_slice_in_dim(t, rank * block, block)
-    partial = jnp.sum(distribution, axis=2)
-    copies = lax.all_to_all(
-        jnp.broadcast_to(partial[None], (groups, rows, cols)), "vel", 0, 0, tiled=True
-    )
-    density = jnp.sum(copies, axis=0)
-    fluid = (cell_type == 0)[:, :, None]
-    wall = jnp.where(cell_type[:, :, None] == 1, here(still)[None, None, :], here(moving)[None, None, :])
-    walled = jnp.where(fluid, distribution, density[:, :, None] * wall)
-    count = lax.axis_size("cell")
-    up = [(i, i + 1) for i in range(count - 1)]
-    below = lax.ppermute(walled[:, cols - 1 :], "cell", up)
-    above = lax.ppermute(walled[:, :1], "cell", [(b, a) for a, b in up])
-    rimmed = jnp.concatenate([below, walled, above], axis=1)
-    padded = jnp.pad(rimmed, ((1, 1), (0, 0), (0, 0)))
-    moved = jnp.where(fluid, walled + transport(padded, here(along_x), here(along_y)), walled)
-    types = lax.dynamic_slice_in_dim(cell_type, rank * slab, slab, 0)
+    )(distribution, cell_type, index, profiles, first, second, loss, *tables)
+
+
+def on_device(lines, tables, index, profiles, distribution, cell_type, first, second, loss):
     done = step(
-        moved.reshape(groups, CHUNKS, CELLS, block),
-        types.reshape(CHUNKS, CELLS, 1),
-        one_hot,
+        distribution.reshape(1024, 512),
+        cell_type.T,
+        index,
+        profiles,
         first,
         second,
-        jnp.broadcast_to(loss[None], (8, 4096)),
+        loss.reshape(1, 4096),
         lines,
         tables,
     )
-    return done.reshape(rows, cols, block)
+    return done.reshape(distribution.shape)
 
 
 def solution(mesh):
-    lines, tables, one_hot = constant_tables()
+    lines, tables, index = constant_tables()
 
     def body(*arguments):
-        return on_device(lines, tables, jnp.asarray(one_hot), *arguments)
+        return on_device(lines, tables, index, cell_rows(), *arguments)
 
     return jax.shard_map(
         body,

time: 99.1 us -> 85.1 us (0.86)
  Pallas kernels: 62.8 us -> 81.9 us
  starting transfers between devices: 13.5 us -> 0 us
  waiting for transfers between devices: 9.42 us -> 0 us
  other arithmetic: 8.66 us -> 0 us
  local copies, waits for them, and re-layouts: 4.26 us -> 3.08 us
    pallas_call x1, Pallas kernels: 62.8 us -> 81.9 us  [step(): pl.pallas_call(functools.partial(step_body, *lines), out_shape=jax.ShapeD...]
    ppermute x2 -> x0, starting transfers between devices: 8.44 us -> none  [the longest x1 6.52 us: on_device(): below = lax.ppermute(walled[:, cols - 1:], 'cell', up)]
    ppermute x2 -> x0, waiting for transfers between devices: 7.03 us -> none  [the longest x1 5.9 us: on_device(): above = lax.ppermute(walled[:, :1], 'cell', [(b, a) for a, b in up])]
    all_to_all x1 -> x0, starting transfers between devices: 5.03 us -> none  [on_device(): lax.all_to_all(jnp.broadcast_to(partial[None], (groups, rows, cols)), 've...]
    select_n x2 -> x0, other arithmetic: 4.25 us -> none  [the longest x1 2.98 us: on_device(): walled = jnp.where(fluid, distribution, density[:, :, None] * wall)]
    reduce_sum x3 -> x0, other arithmetic: 2.58 us -> none  [the longest x1 1.82 us: on_device(): partial = jnp.sum(distribution, axis=2)]
    all_to_all x1 -> x0, waiting for transfers between devices: 2.4 us -> none  [on_device(): lax.all_to_all(jnp.broadcast_to(partial[None], (groups, rows, cols)), 've...]
    max x1 -> x0, other arithmetic: 1.39 us -> none  [transport(): plus_x = jnp.maximum(along_x, 0.0)[None, None, :]]
  transfers between devices with their start and end apart: 3 -> 0, of which waited for: 3 -> 0; matrix products, arithmetic and copies ran while one was open for 3% -> 0% of each run, Pallas kernels for 0% -> 0%
where the time goes in v3:
time: 85.1 us; the launch traced here: 84.9 us
  Pallas kernels  81.9 us (96%)
  local copies, waits for them, and re-layouts  3.08 us (4%)
    pallas_call x1, Pallas kernels, step(): pl.pallas_call(functools.partial(step_body, *lines), out_shape=jax.ShapeD...  81.9 us
    unnamed x1, local copies, waits for them, and re-layouts  3.08 us

profile of v3, /device:TPU:33, one launch (start us, length us, event | category | flops | bytes accessed | tf_op | source)
XLA Modules:
  0.0 84.9 jit_solution(13219076090189581867)
XLA Ops:
  0.0 81.9 %step.1 = f32[8,2,64,512]{3,2,1,0:T(8,128)} custom-call(f32[1024,512]{1,0:T(8,128)} %bitcast.5, s32[8,128]{1,0:T(8,128)} %bitcast.7, s32[4,2,256]{2,1,0:T(2,128)} %constant.12.clone.index_ref, f32[8,8,512]{2,1,0:T(8,128)} %constant.13.clone.rows_hbm, f32[16,4096]{1,0:T(8,128)} %first_ref.1, f32[16,4096]{1,0:T(8,128)} %second_ref.1, f32[1,4096]{1,0:T(1,128)} %bitcast.6, ...), custom_call_target="tpu_custom_call" | custom-call | tf_op jit(solution)/shard_map/step/pallas_call | solution.py:491
  81.9 3.1 %copy.13 = f32[128,8,512]{2,1,0:T(8,128)} copy(f32[128,8,512]{2,1,0:T(8,128)} %bitcast.4) | data formatting | bytes 4194304

commit v4 on v3

--- a/solution.py
+++ b/solution.py
@@ -174,8 +174,8 @@
         return 0
 
     lax.fori_loop(0, CELLS // 16, rows, 0)
-    wide = 4 * CELLS
-    for first, size in ((0, wide), (wide, wide), (2 * wide, CELLS)):
+    wide = 8 * CELLS
+    for first, size in ((0, wide), (wide, CELLS)):
         part = x1_ref[first : first + size, :]
         o = lax.dot_general(jt_ref[...], part, NT, preferred_element_type=F32)
         x2_ref[:, first : first + size] = o.astype(BF16)
@@ -185,21 +185,26 @@
             kt_ref[kind], x2_ref[:, first : first + size], NN, preferred_element_type=F32
         )
         for t, a in enumerate(places):
-            v = o[:, t * CELLS : t * CELLS + CELLS].astype(BF16)
-            sr_ref[:, a * 16 : a * 16 + 16, :] = v.reshape(N, 16, CELLS)
-
-    put(1, 0, wide, (1, 2, 3, 4))
-    put(3, 0, wide, (15, 14, 13, 12))
-    put(1, wide, wide, (5, 6, 7))
-    put(3, wide, wide, (11, 10, 9))
-    put(2, wide + 3 * CELLS, CELLS, (8,))
-    put(0, 2 * wide, CELLS, (0,))
-    for row in range(N):
-        s_ref[row] = sr_ref[row].astype(F32).T
-
-
-CHUNKS = 2
+            v = o[:, t * CELLS : t * CELLS + CELLS].astype(BF16).reshape(N, 16, CELLS)
+            for row in range(N):
+                at = row % CHUNKS * CELLS
+                sr_ref[row // CHUNKS, a * 16 : a * 16 + 16, at : at + CELLS] = v[row]
+
+    put(1, 0, wide, (1, 2, 3, 4, 5, 6, 7))
+    put(3, 0, wide, (15, 14, 13, 12, 11, 10, 9))
+    put(2, 7 * CELLS, CELLS, (8,))
+    put(0, wide, CELLS, (0,))
+    for t in range(N // CHUNKS):
+        s_ref[CHUNKS * t : CHUNKS * t + CHUNKS] = sr_ref[t].astype(F32).T.reshape(CHUNKS, CELLS, 256)
+
+
+CHUNKS = 4
 CELLS = 128 // CHUNKS
+ROWS = CELLS // 8
+NEED = [
+    [15] * (c == 0) + [u for u in range(c * ROWS + (c > 0), c * ROWS + ROWS + 1) if u < 15]
+    for c in range(CHUNKS)
+]
 GROUP = 8
 
 
@@ -231,9 +236,9 @@
 def step_body(
     fr, fi, dist_ref, type_ref, index_ref, rows_hbm, first_ref, second_ref, loss_ref,
     jt_hbm, kt_hbm, ib_hbm, ia_hbm, out_ref,
-    d_ref, w_ref, t_ref, e_ref, h_ref, msg_ref, in_ref, row_ref, moved_ref,
+    d_ref, w_ref, t_ref, e_ref, h_ref, side_ref, msg_ref, in_ref, row_ref, moved_ref,
     x_ref, r_ref, all_ref, mid_ref, hot_ref, k_ref, jt_ref, kt_ref, ib_ref, ia_ref,
-    x1_ref, x2_ref, sr_ref, s_ref, z_ref, g_ref,
+    x1_ref, x2_ref, sr_ref, s_ref, zl_ref, l_ref, z_ref, g_ref,
     send_sem, recv_sem, back_send, back_recv, own_sem, load_sem,
     dist_sem, msg_send, msg_recv, edge_send, edge_recv,
 ):
@@ -286,7 +291,8 @@
             total = jnp.where(lane == x, jnp.sum(v, axis=1, keepdims=True), total)
             for side in range(2):
                 at = x * 8 + 7 * side
-                e_ref[side, x : x + 1, :] = d_ref[at : at + 1, :]
+                place = t * ROWS + u % ROWS
+                e_ref[side, u // ROWS, place : place + 1, :] = d_ref[at : at + 1, :]
     kinds = type_ref[...].astype(F32)
     msg_ref[0:8, :] = total
     msg_ref[8:16, :] = kinds
@@ -300,7 +306,11 @@
         )
 
     edges = [
-        reach(e_ref.at[side], h_ref.at[1 - side], edge_send.at[side], edge_recv.at[side], sides[side], me)
+        reach(
+            e_ref.at[side, c], h_ref.at[1 - side, c], edge_send.at[side, c], edge_recv.at[side, c],
+            sides[side], me,
+        )
+        for c in range(CHUNKS)
         for side in range(2)
     ]
     notes = []
@@ -314,15 +324,24 @@
                         place, peer,
                     )
                 )
-    for copy in edges + notes:
+    for copy in edges[:2] + notes + edges[2:]:
         copy.start()
+
+    def types(t, _):
+        for u in range(8):
+            x = t * 8 + u
+            kind = jnp.sum(jnp.where(lane == x, kinds, 0.0), axis=1, keepdims=True)
+            t_ref[pl.ds(pl.multiple_of(x * 8, 8), 8), :] = jnp.broadcast_to(kind, (8, 128))
+        return 0
+
+    lax.fori_loop(0, 16, types, 0)
 
     for copy in loads:
         copy.wait()
     all_ref[32:48] = jnp.broadcast_to(loss_ref[...], (16, 4096))
     pack(index_ref, all_ref, mid_ref, hot_ref, k_ref)
     profile.wait()
-    for copy in notes + edges:
+    for copy in notes:
         copy.wait()
     still, moving = row_ref[4:5, :], row_ref[5:6, :]
 
@@ -332,39 +351,55 @@
         return (v[0] + v[1])[0:8]
 
     for side in range(2):
-        density = gathered(1 + side).T[:, 7 - 7 * side : 8 - 7 * side]
-        kind = in_ref[1 + side, 0, 8:16, :].T[:, 7 - 7 * side : 8 - 7 * side]
-        wall = density * jnp.where(kind == 1.0, still, moving)
-        inside = cell > 0 if side == 0 else cell < cells - 1
-        h_ref[side] = jnp.where(kind == 0.0, h_ref[side], wall) * jnp.where(inside, 1.0, 0.0)
+        edge = slice(7 - 7 * side, 8 - 7 * side)
+        sums = jnp.broadcast_to(gathered(1 + side)[edge], (8, 128))
+        side_ref[side, 0] = sums.T
+        side_ref[side, 1] = jnp.broadcast_to(in_ref[1 + side, 0, 8:16, :][edge], (8, 128)).T
+
+    def halo(c):
+        for side in range(2):
+            edges[2 * c + side].wait()
+        for side in range(2):
+            column = [
+                jnp.concatenate(
+                    [side_ref[side, k, d * 16 + c * ROWS : d * 16 + c * ROWS + ROWS, :] for d in range(GROUP)],
+                    axis=0,
+                )[:, 0:1]
+                for k in range(2)
+            ]
+            wall = column[0] * jnp.where(column[1] == 1.0, still, moving)
+            inside = cell > 0 if side == 0 else cell < cells - 1
+            raw = h_ref[side, c]
+            h_ref[side, c] = jnp.where(column[1] == 0.0, raw, wall) * jnp.where(inside, 1.0, 0.0)
+
     density = gathered(0)
     w_ref[0:8, :] = jnp.zeros((8, 512), F32)
     w_ref[1032:1040, :] = jnp.zeros((8, 512), F32)
 
-    def walled(t, _):
-        for u in range(8):
-            x = t * 8 + u
-            at = pl.ds(pl.multiple_of(x * 8, 8), 8)
-            here = lane == x
-            kind = jnp.sum(jnp.where(here, kinds, 0.0), axis=1, keepdims=True)
-            dense = jnp.sum(jnp.where(here, density, 0.0), axis=1, keepdims=True)
-            wall = dense * jnp.where(kind == 1.0, still, moving)
-            w = jnp.where(kind == 0.0, d_ref[at, :], wall)
-            w_ref[pl.ds(pl.multiple_of(x * 8 + 8, 8), 8), :] = w
-            t_ref[at, :] = jnp.broadcast_to(kind, (8, 128))
-        return 0
-
-    lax.fori_loop(0, 16, walled, 0)
+    def walled(rows):
+        def body(t, _):
+            for u in rows:
+                x = t * 16 + u
+                at = pl.ds(pl.multiple_of(x * 8, 8), 8)
+                kind = jnp.concatenate([t_ref[at, :]] * 4, axis=1)
+                dense = jnp.sum(jnp.where(lane == x, density, 0.0), axis=1, keepdims=True)
+                wall = dense * jnp.where(kind == 1.0, still, moving)
+                w = jnp.where(kind == 0.0, d_ref[at, :], wall)
+                w_ref[pl.ds(pl.multiple_of(x * 8 + 8, 8), 8), :] = w
+            return 0
+
+        lax.fori_loop(0, GROUP, body, 0)
+
     depth = lax.broadcasted_iota(jnp.int32, (8, 512), 0)
 
     def transport(peer, c, out_ref, *place):
-        for u in range(8):
-            x = peer * 16 + c * 8 + u
+        for u in range(ROWS):
+            x = peer * 16 + c * ROWS + u
             low = w_ref[pl.ds(pl.multiple_of(x * 8, 8), 8), :]
             w = w_ref[pl.ds(pl.multiple_of(x * 8 + 8, 8), 8), :]
             high = w_ref[pl.ds(pl.multiple_of(x * 8 + 16, 8), 8), :]
-            left = jnp.where(depth == 0, h_ref[0, pl.ds(x, 1), :], pltpu.roll(w, 1, 0))
-            right = jnp.where(depth == 7, h_ref[1, pl.ds(x, 1), :], pltpu.roll(w, 7, 0))
+            left = jnp.where(depth == 0, h_ref[0, c, pl.ds(peer * ROWS + u, 1), :], pltpu.roll(w, 1, 0))
+            right = jnp.where(depth == 7, h_ref[1, c, pl.ds(peer * ROWS + u, 1), :], pltpu.roll(w, 7, 0))
             flow = row_ref[0:1, :] * (w - low) + row_ref[1:2, :] * (high - w)
             flow = flow + row_ref[2:3, :] * (w - left) + row_ref[3:4, :] * (right - w)
             kind = t_ref[pl.ds(pl.multiple_of(x * 8, 8), 8), :]
@@ -377,27 +412,20 @@
             moved_ref.at[c, peer], x_ref.at[c, me], send_sem.at[c, s], recv_sem.at[c, s], peer
         )
 
-    def first_half(s, _):
-        peer = lax.rem(me + s, GROUP)
-        transport(peer, 0, moved_ref, 0, peer)
-        send(0, s).start()
-        return 0
-
-    def second_half(s, _):
-        peer = lax.rem(me + s, GROUP)
-        transport(peer, 1, moved_ref, 1, peer)
-        return 0
-
-    lax.fori_loop(1, GROUP, first_half, 0)
-    lax.fori_loop(1, GROUP, second_half, 0)
     for c in range(CHUNKS):
+        walled(NEED[c])
+        halo(c)
+
+        def part(s, _):
+            peer = lax.rem(me + s, GROUP)
+            transport(peer, c, moved_ref, c, peer)
+            send(c, s).start()
+            return 0
+
+        lax.fori_loop(1, GROUP, part, 0)
         transport(me, c, x_ref, c, me)
     for copy in tables:
         copy.wait()
-    for s in range(1, GROUP):
-        send(0, s).wait_send()
-    for s in range(1, GROUP):
-        send(1, s).start()
 
     def chunk(c, _):
         for s in range(1, GROUP):
@@ -432,32 +460,34 @@
         for row in range(N):
             one = (s_ref[row] * k_ref[row, 32:33, :]).astype(BF16)
             kind = 1 if row % 8 == 0 else 0
-            o = lax.dot_general(ib_ref[kind], one, NT, preferred_element_type=F32)
-            z_ref[:, row * 16 : row * 16 + 16, :CELLS] = o.astype(BF16).reshape(N, 16, CELLS)
+            o = lax.dot_general(
+                ib_ref[kind], jnp.concatenate([one] * CHUNKS, axis=0), NT, preferred_element_type=F32
+            ).astype(BF16)
+            for i in range(N):
+                lanes = slice(i % CHUNKS * CELLS, i % CHUNKS * CELLS + CELLS)
+                zl_ref[i // CHUNKS, row * 16 : row * 16 + 16, lanes] = o[i * 16 : i * 16 + 16, lanes]
+        for t in range(N // CHUNKS):
+            o = lax.dot_general(ia_ref[...], zl_ref[t], NN, preferred_element_type=F32)
+            l_ref[CHUNKS * t : CHUNKS * t + CHUNKS] = o.T.reshape(CHUNKS, CELLS, 256)
         at = pl.ds(pl.multiple_of(me * 128 + c * CELLS, CELLS), CELLS)
         fluid = jnp.concatenate([t_ref[at, :]] * 2, axis=1) == 0.0
 
         def finish(peer):
             for h in range(2):
                 i = 2 * peer + h
-                loss = lax.dot_general(
-                    ia_ref[...], z_ref[i, :, :CELLS], NN, preferred_element_type=F32
-                )
                 gain = g_ref[i].T
-                gain = gain[:CELLS] + gain[CELLS:]
+                gain = sum(gain[t * CELLS : t * CELLS + CELLS] for t in range(CHUNKS))
                 x = x_ref[c, peer, :, h * 256 : h * 256 + 256]
-                change = gain - x * loss.T
+                change = gain - x * l_ref[i]
                 r_ref[c, peer, :, h * 256 : h * 256 + 256] = jnp.where(
                     fluid, x + collision_timestep * change, x
                 )
 
-        def one(s, _):
-            peer = lax.rem(me + s, GROUP)
-            finish(peer)
-            back(c, s).start()
-            return 0
-
-        lax.fori_loop(1, GROUP, one, 0)
+        for group in ((1, 2, 3), (4, 5, 6, 7)):
+            for s in group:
+                finish(lax.rem(me + s, GROUP))
+            for s in group:
+                back(c, s).start()
         finish(me)
         pltpu.make_async_copy(r_ref.at[c, me], out_ref.at[me, c], own_sem.at[c]).start()
         return 0
@@ -472,8 +502,7 @@
     for c in range(CHUNKS):
         pltpu.make_async_copy(r_ref.at[c, me], out_ref.at[me, c], own_sem.at[c]).wait()
         for s in range(1, GROUP):
-            if c:
-                send(c, s).wait_send()
+            send(c, s).wait_send()
             back(c, s).wait()
 
 
@@ -492,13 +521,14 @@
         functools.partial(step_body, *lines),
         out_shape=jax.ShapeDtypeStruct((GROUP, CHUNKS, CELLS, 512), F32),
         in_specs=[hbm, vmem, vmem] + [hbm] * 3 + [vmem] + [hbm] * 4,
-        out_specs=hbm,
+        out_specs=vmem,
         scratch_shapes=[
             pltpu.VMEM((1024, 512), F32),
             pltpu.VMEM((1040, 512), F32),
             pltpu.VMEM((1024, 128), F32),
-            pltpu.VMEM((2, 128, 512), F32),
-            pltpu.VMEM((2, 128, 512), F32),
+            pltpu.VMEM((2, CHUNKS, 8 * ROWS, 512), F32),
+            pltpu.VMEM((2, CHUNKS, 8 * ROWS, 512), F32),
+            pltpu.VMEM((2, 2, 128, 8), F32),
             pltpu.VMEM((16, 128), F32),
             pltpu.VMEM((3, GROUP, 16, 128), F32),
             pltpu.VMEM((8, 512), F32),
@@ -515,7 +545,9 @@
             pltpu.VMEM((256, 256), BF16),
             pltpu.VMEM((9 * CELLS, 512), BF16),
             pltpu.VMEM((512, 9 * CELLS), BF16),
-            pltpu.VMEM((N, 256, CELLS), BF16),
+            pltpu.VMEM((N // CHUNKS, 256, 128), BF16),
+            pltpu.VMEM((N, CELLS, 256), F32),
+            pltpu.VMEM((N // CHUNKS, 256, 128), BF16),
             pltpu.VMEM((N, CELLS, 256), F32),
             pltpu.VMEM((N, 256, 256), BF16),
             pltpu.VMEM((N, 256, 128), F32),
@@ -528,8 +560,8 @@
             dma((GROUP,)),
             dma((3, GROUP)),
             dma((3, GROUP)),
-            dma((2,)),
-            dma((2,)),
+            dma((2, CHUNKS)),
+            dma((2, CHUNKS)),
         ],
         compiler_params=pltpu.CompilerParams(
             vmem_limit_bytes=62 << 20, collective_id=0, has_side_effects=True

time: 85.1 us -> 74.4 us (0.87); the launches traced: 84.9 us -> 73.1 us
  Pallas kernels: 81.9 us -> 70 us
    pallas_call x1, Pallas kernels: 81.9 us -> 70 us  [step(): pl.pallas_call(functools.partial(step_body, *lines), out_shape=jax.ShapeD...]
where the time goes in v4:
time: 74.4 us; the launch traced here: 73.1 us
  Pallas kernels  70 us (94%)
  local copies, waits for them, and re-layouts  3.08 us (4%)
    pallas_call x1, Pallas kernels, step(): pl.pallas_call(functools.partial(step_body, *lines), out_shape=jax.ShapeD...  70 us
    unnamed x1, local copies, waits for them, and re-layouts  3.08 us

profile of v4, /device:TPU:33, one launch (start us, length us, event | category | flops | bytes accessed | tf_op | source)
XLA Modules:
  0.0 73.1 jit_solution(8077464791635584687)
XLA Ops:
  0.0 70.0 %step.1 = f32[8,4,32,512]{3,2,1,0:T(8,128)} custom-call(f32[1024,512]{1,0:T(8,128)} %bitcast.5, s32[8,128]{1,0:T(8,128)} %bitcast.7, s32[4,2,256]{2,1,0:T(2,128)} %constant.12.clone.index_ref, f32[8,8,512]{2,1,0:T(8,128)} %constant.13.clone.rows_hbm, f32[16,4096]{1,0:T(8,128)} %first_ref.1, f32[16,4096]{1,0:T(8,128)} %second_ref.1, f32[1,4096]{1,0:T(1,128)} %bitcast.6, ...), custom_call_target="tpu_custom_call" | custom-call | tf_op jit(solution)/shard_map/step/pallas_call | solution.py:520
  70.0 3.1 %copy.13 = f32[128,8,512]{2,1,0:T(8,128)} copy(f32[128,8,512]{2,1,0:T(8,128)} %bitcast.4) | data formatting | bytes 4194304

commit v5 on v4

--- a/solution.py
+++ b/solution.py
@@ -339,7 +339,6 @@
     for copy in loads:
         copy.wait()
     all_ref[32:48] = jnp.broadcast_to(loss_ref[...], (16, 4096))
-    pack(index_ref, all_ref, mid_ref, hot_ref, k_ref)
     profile.wait()
     for copy in notes:
         copy.wait()
@@ -424,6 +423,8 @@
 
         lax.fori_loop(1, GROUP, part, 0)
         transport(me, c, x_ref, c, me)
+        if c == 1:
+            pack(index_ref, all_ref, mid_ref, hot_ref, k_ref)
     for copy in tables:
         copy.wait()
 
@@ -521,7 +522,7 @@
         functools.partial(step_body, *lines),
         out_shape=jax.ShapeDtypeStruct((GROUP, CHUNKS, CELLS, 512), F32),
         in_specs=[hbm, vmem, vmem] + [hbm] * 3 + [vmem] + [hbm] * 4,
-        out_specs=vmem,
+        out_specs=pl.BlockSpec(memory_space=pl.ANY),
         scratch_shapes=[
             pltpu.VMEM((1024, 512), F32),
             pltpu.VMEM((1040, 512), F32),

time: 74.4 us -> 72.7 us (0.977)
  Pallas kernels: 70 us -> 68.2 us
    pallas_call x1, Pallas kernels: 70 us -> 68.2 us  [step(): pl.pallas_call(functools.partial(step_body, *lines), out_shape=jax.ShapeD...]
where the time goes in v5:
time: 72.7 us; the launch traced here: 71.3 us
  Pallas kernels  68.2 us (94%)
  local copies, waits for them, and re-layouts  3.08 us (4%)
    pallas_call x1, Pallas kernels, step(): pl.pallas_call(functools.partial(step_body, *lines), out_shape=jax.ShapeD...  68.2 us
    unnamed x1, local copies, waits for them, and re-layouts  3.08 us

profile of v5, /device:TPU:33, one launch (start us, length us, event | category | flops | bytes accessed | tf_op | source)
XLA Modules:
  0.0 71.3 jit_solution(14247642344888203884)
XLA Ops:
  0.0 68.2 %step.1 = f32[8,4,32,512]{3,2,1,0:T(8,128)} custom-call(f32[1024,512]{1,0:T(8,128)} %bitcast.5, s32[8,128]{1,0:T(8,128)} %bitcast.7, s32[4,2,256]{2,1,0:T(2,128)} %constant.12.clone.index_ref, f32[8,8,512]{2,1,0:T(8,128)} %constant.13.clone.rows_hbm, f32[16,4096]{1,0:T(8,128)} %first_ref.1, f32[16,4096]{1,0:T(8,128)} %second_ref.1, f32[1,4096]{1,0:T(1,128)} %bitcast.6, ...), custom_call_target="tpu_custom_call" | custom-call | tf_op jit(solution)/shard_map/step/pallas_call | solution.py:521
  68.2 3.1 %copy.13 = f32[128,8,512]{2,1,0:T(8,128)} copy(f32[128,8,512]{2,1,0:T(8,128)} %bitcast.4) | data formatting | bytes 4194304
